TPU v7x, 256 devices: a whole 4x4x8 slice. The times are simulated.
256 devices in a mesh: gx: 128 (over x, y, z), gy: 2 (over core).
Axes of the slice: x: 4, y: 4, z: 8, core: 2. Of those that a mesh axis runs over, the one named last changes fastest.
Arguments:
- positions: float32 [3, 2, 1114112], P(None, 'gy', 'gx'), may hold values from -7 to 7
- forces: float32 [3, 2, 1114112], P(None, 'gy', 'gx'), may hold values from -6 to 6
- deriv_mat: float32 [544, 544], replicated, may hold values from -0.25 to 0.25
- quad_mat: float32 [544, 544], replicated, may hold values from -0.25 to 0.25
- point_dest: int32 [2, 1114112], P('gy', 'gx'), may hold values from 0 to 32767, as said below
- leaf_center: float32 [3, 2, 32768], P(None, 'gy', 'gx'), may hold values from -4 to 4
- tile_src: int32 [2, 4194304], P('gy', 'gx'), may hold values from 0 to 32768, as said below
- neighbours: int32 [2, 3, 32768], P('gy', None, 'gx'), may hold values from 0 to 32767, as said below
- inter_leaf: int32 [2, 8, 32768], P('gy', None, 'gx'), may hold values from 0 to 32767, as said below
- inter_op: int32 [2, 8, 32768], P('gy', None, 'gx'), may hold values from 0 to 15
- coarse_op: int32 [2, 128, 256], P('gy', 'gx'), may hold values from 0 to 16, as said below
- up_pinv: float32 [168, 168], replicated, may hold values from -0.5 to 0.5
- trans_ops: float32 [16, 168, 168], replicated, may hold values from -0.25 to 0.25
- child_ops: float32 [8, 168, 168], replicated, may hold values from -0.03125 to 0.03125
Outputs:
- velocity: float32 [3, 2, 1114112], P(None, 'gy', 'gx')
Inputs may be any that keep to these rules, and one draw needn't show every extreme that they name: `point_dest`: within one slab and one column block d, the values are distinct; the slots sent to each owner are used from k = 0 without gaps; every column block fills all 256 slots of the same 128 // 8 owners. `tile_src`: each point of the slab fills exactly one leaf slot of the owner it is sent to; 32768 marks an empty slot; the busiest owners have all slots filled. `neighbours`: entry 0 is the leaf itself; the others lie within 256 leaves of it. `inter_leaf`: every entry lies within 256 leaves of its leaf. `coarse_op`: 16 marks no interaction; it stands exactly for the target box itself and the boxes of the owners next to it in the same slab.
All inputs are finite; a program needn't handle non-finite values.
Results may differ from a plain program's by a relative error of at most 0.0003.
Values sent between devices are 32-bit elements; how exact they have to be, the bound alone decides.
No kernel may reach another device: no remote copies, remote signals or barrier semaphores. Data moves between devices by JAX's collectives and lax.ppermute only.
A program may use at most 192 MiB of HBM per device.

v0:
```python
import math

import jax
import jax.numpy as jnp
from jax import lax
from jax.sharding import Mesh
from jax.sharding import PartitionSpec as P

P_SIZE = 544
NOPS = 16
TILE = 128
L_DEV = 256
GX = ("gx_0", "gx_1", "gx_2")
GX_GY = ("gx_0", "gx_1", "gx_2", "gy")


SOFTENING = 0.25
RADIUS = 2.5
HIGHEST = lax.Precision.HIGHEST


def extended_2(shard, sides, width):
    for axis, dim in sides:
        devices, length = (lax.axis_size(axis), shard.shape[dim])
        up = [(i, (i + 1) % devices) for i in range(devices - 1)]
        down = [(j, i) for i, j in up]
        last = lax.slice_in_dim(shard, length - width, length, axis=dim)
        first = lax.slice_in_dim(shard, 0, width, axis=dim)
        before = lax.ppermute(last, axis, up)
        after = lax.ppermute(first, axis, down)
        shard = jnp.concatenate([before, shard, after], axis=dim)
    return shard


def joined_along(tiles, dim):
    tiles = jnp.moveaxis(tiles, 0, dim)
    dims = tiles.shape
    return tiles.reshape(*dims[:dim], dims[dim] * dims[dim + 1], *dims[dim + 2 :])


def all_blocks(shard, axes, order):
    tiles = shard[None]
    for k in order:
        tiles = lax.all_gather(tiles, axes[k], axis=0, tiled=True)
    held = [lax.axis_size(axes[k]) for k in reversed(order)]
    tiles = tiles.reshape(*held, *shard.shape)
    turned = sorted(range(len(order)), key=lambda place: order[len(order) - 1 - place])
    return tiles.transpose(*turned, *range(len(order), tiles.ndim)).reshape(-1, *shard.shape)


def gather_axes(shard, axes, order, dim):
    return joined_along(all_blocks(shard, axes, order), dim)


def sphere_points(count):
    index = jnp.arange(count).astype(jnp.float32)
    height = 1.0 - (2.0 * index + 1.0) / count
    radial = jnp.sqrt(1.0 - height * height)
    angle = 2.399963 * index
    return jnp.stack([radial * jnp.cos(angle), radial * jnp.sin(angle), height])


def stokes_sum(targets, sources, strengths):
    delta_x = targets[0][:, :, None] - sources[0][:, None, :]
    delta_y = targets[1][:, :, None] - sources[1][:, None, :]
    delta_z = targets[2][:, :, None] - sources[2][:, None, :]
    soft_sq = delta_x * delta_x + delta_y * delta_y + delta_z * delta_z + SOFTENING
    inverse = 1.0 / (soft_sq * jnp.sqrt(soft_sq))
    push_x = strengths[0][:, None, :]
    push_y = strengths[1][:, None, :]
    push_z = strengths[2][:, None, :]
    projected = (push_x * delta_x + push_y * delta_y + push_z * delta_z) * inverse
    direct = (soft_sq + SOFTENING) * inverse
    return jnp.stack(
        [
            jnp.sum(push_x * direct + projected * delta_x, axis=2),
            jnp.sum(push_y * direct + projected * delta_y, axis=2),
            jnp.sum(push_z * direct + projected * delta_z, axis=2),
        ]
    )


def by_blocks(func, arrays, total, width):

    def one_block(start):
        return func(*[lax.dynamic_slice_in_dim(item, start, width, 1) for item in arrays])

    starts = jnp.arange(total // width) * width
    result = lax.map(one_block, starts)
    return jnp.transpose(result, (1, 0, 2, 3)).reshape(result.shape[1], total, result.shape[3])


def moments(tiles, centers, sphere, up_pinv, width):
    total = centers.shape[1]
    checks = centers[:, :, None] + RADIUS * sphere[:, None, :]
    values = by_blocks(stokes_sum, [checks, tiles[:3], tiles[3:]], total, width)
    stacked = jnp.transpose(values, (0, 2, 1)).reshape(-1, total)
    return jnp.dot(up_pinv.T, stacked, precision=HIGHEST, preferred_element_type=jnp.float32)


def children(multipole, child_ops):
    expansion = multipole.shape[0]
    grouped = jnp.sum(multipole.reshape(expansion, -1, L_DEV // 8, 8), axis=2)
    return jnp.einsum("cef,ebc->bf", child_ops, grouped, precision=HIGHEST)


def coarse_terms(op_rows, coarse):
    onehot = (op_rows[:, :, None] == jnp.arange(NOPS)[None, None, :]).astype(jnp.float32)
    return jnp.einsum("tbk,be->tke", onehot, coarse, precision=HIGHEST)


def translate(trans_ops, grouped):
    return jnp.einsum("kef,tke->tf", trans_ops, grouped, precision=HIGHEST)


def leaf_translate(extended, index, op_rows, trans_ops):
    picked = extended[:, index]
    onehot = (op_rows[:, :, None] == jnp.arange(NOPS)[None, None, :]).astype(jnp.float32)
    grouped = jnp.einsum("ejn,jnk->ken", picked, onehot, precision=HIGHEST)
    return jnp.einsum("kef,ken->fn", trans_ops, grouped, precision=HIGHEST)


def downward(coarse_local, child_ops, leaves):
    pushed = jnp.einsum("cfe,be->fbc", child_ops, coarse_local, precision=HIGHEST)
    expansion = pushed.shape[0]
    boxes = pushed.shape[1]
    spread = jnp.broadcast_to(pushed[:, :, None, :], (expansion, boxes, leaves // 8, 8))
    return spread.reshape(expansion, boxes * leaves)


def evaluate(tiles, centers, sphere, local, width):
    total = centers.shape[1]
    surface = centers[:, :, None] + RADIUS * sphere[:, None, :]
    density = jnp.transpose(local.reshape(3, -1, total), (0, 2, 1))
    return by_blocks(stokes_sum, [tiles[:3], surface, density], total, width)


def pick_slots(arrived, table):
    flat = arrived.reshape(arrived.shape[0], -1)
    rows_view = jnp.concatenate([flat.T, jnp.zeros((1, flat.shape[0]), jnp.float32)], axis=0)
    return jnp.take(rows_view, table, axis=0).T


def place_rows(values, where, length):
    rows_view = jnp.zeros((length + 1, values.shape[0]), jnp.float32).at[where].set(values.T)
    return rows_view[:length].T


def body(
    positions,
    forces,
    deriv_mat,
    quad_mat,
    point_dest,
    leaf_center,
    tile_src,
    neighbours,
    inter_leaf,
    inter_op,
    coarse_op,
    up_pinv,
    trans_ops,
    child_ops,
):
    owners = lax.axis_size(GX)
    count = positions.shape[2]
    leaves = leaf_center.shape[2]
    slots = leaves * TILE
    capacity = slots // owners
    tangent = jnp.dot(
        positions.reshape(-1, P_SIZE),
        deriv_mat,
        precision=HIGHEST,
        preferred_element_type=jnp.float32,
    ).reshape(3, count)
    jacobian = jnp.sqrt(1.0 + jnp.sum(tangent * tangent, axis=0))
    weighted = jnp.dot(
        forces.reshape(-1, P_SIZE), quad_mat, precision=HIGHEST, preferred_element_type=jnp.float32
    ).reshape(3, count)
    packed = jnp.concatenate([positions.reshape(3, count), weighted * jacobian[None]], axis=0)
    outgoing = place_rows(packed, point_dest[0], owners * capacity).reshape(6, owners, capacity)
    first = lax.axis_index(GX) * leaves - leaves
    arrived = lax.all_to_all(outgoing, GX, split_axis=1, concat_axis=1, tiled=True)
    owned = pick_slots(arrived, tile_src[0])
    extended = extended_2(owned, ((GX, 1),), slots)
    sphere = sphere_points(up_pinv.shape[0] // 3)
    width = min(16, leaves)
    leaf_major = jnp.transpose(extended.reshape(6, 3 * leaves, TILE), (1, 0, 2))
    owned_tiles = owned.reshape(6, leaves, TILE)
    gathered = jnp.take(leaf_major, neighbours[0].T - first, axis=0)
    picked = jnp.transpose(gathered, (2, 0, 1, 3)).reshape(6, leaves, -1)
    near = by_blocks(stokes_sum, [owned_tiles[:3], picked[:3], picked[3:]], leaves, width)
    centers = leaf_center[:, 0]
    multipole = moments(owned_tiles, centers, sphere, up_pinv, width)
    multipole_ext = extended_2(multipole, ((GX, 1),), leaves)
    local = leaf_translate(multipole_ext, inter_leaf[0] - first, inter_op[0], trans_ops)
    box_moment = children(multipole, child_ops)
    op_row = coarse_op[0]
    grouped = coarse_terms(op_row, gather_axes(box_moment, GX_GY, (0, 1, 2, 3), 0))
    local = local + downward(translate(trans_ops, grouped), child_ops, leaves)
    far = evaluate(owned_tiles, centers, sphere, local, width)
    flow = ((near + far) / (8.0 * math.pi)).reshape(3, slots)
    returning = place_rows(flow, tile_src[0], owners * capacity)
    came_back = lax.all_to_all(
        returning.reshape(3, owners, capacity), GX, split_axis=1, concat_axis=1, tiled=True
    ).reshape(3, owners * capacity)
    return jnp.take(came_back.T, point_dest[0], axis=0).T.reshape(3, 1, count)


def solution(mesh):
    split = Mesh(mesh.devices.reshape(4, 4, 8, mesh.shape["gy"]), ("gx_0", "gx_1", "gx_2", "gy"))
    in_specs = (
        P(None, "gy", GX),
        P(None, "gy", GX),
        P(),
        P(),
        P("gy", GX),
        P(None, "gy", GX),
        P("gy", GX),
        P("gy", None, GX),
        P("gy", None, GX),
        P("gy", None, GX),
        P("gy", GX, None),
        P(),
        P(),
        P(),
    )
    out_specs = P(None, "gy", GX)
    return jax.shard_map(body, mesh=split, in_specs=in_specs, out_specs=out_specs, check_vma=False)
```

profile of v0, /device:TPU:1, one launch (start us, length us, event | category | flops | bytes accessed | tf_op | source)
XLA Modules:
  0.0 959.0 jit_solution(12978073658870351390)
XLA Ops:
  13.2 28.8 %scatter_custom_fusion = f32[32769,6]{1,0:T(8,128)} fusion(s32[8704]{0:T(1024)S(1)} %get-tuple-element.357, f32[8704,6]{1,0:T(8,128)} %copy.132, f32[]{:T(128)} %constant.196.clone.1), kind=kCustom, calls=%fused_computation.115 | custom fusion | bytes 786968 | tf_op jit(solution)/shard_map/scatter | solution.py:145
  42.0 11.2 %slice.212 = f32[32768,6]{1,0:T(8,128)} slice(f32[32769,6]{1,0:T(8,128)} %scatter_custom_fusion), slice={[0:32768], [0:6]} | slice | bytes 1572864 | tf_op jit(solution)/shard_map/slice | solution.py:146
  53.3 10.1 %copy.133 = f32[6,128,256]{2,0,1:T(8,128)} copy(f32[6,128,256]{0,2,1:T(8,128)} %bitcast.250) | data formatting | bytes 1572864 | tf_op jit(solution)/shard_map/reshape | solution.py:181
  63.4 17.0 %all-to-all-start = ((f32[6,128,256]{2,0,1:T(8,128)}), f32[6,128,256]{2,0,1:T(8,128)}, u32[]{:S(2)}, u32[]{:S(2)}) async-start(f32[6,128,256]{2,0,1:T(8,128)} %copy.133), calls=%async_computation | async-start | bytes 2097152 | tf_op jit(solution)/shard_map/all_to_all | solution.py:183
  85.4 24.9 %all-to-all-done = f32[6,128,256]{2,0,1:T(8,128)} async-done(((f32[6,128,256]{2,0,1:T(8,128)}), f32[6,128,256]{2,0,1:T(8,128)}, u32[]{:S(2)}, u32[]{:S(2)}) %all-to-all-start) | async-done | bytes 786464 | tf_op jit(solution)/shard_map/all_to_all | solution.py:183
  110.3 9.4 copy.134
  119.7 13.3 %concatenate.17 = f32[32769,6]{1,0:T(8,128)} pad(f32[32768,6]{1,0:T(8,128)} %bitcast.249, f32[]{:T(128)} %constant.196.clone.1), padding=0_1x0_0 | pad | bytes 1572892 | tf_op jit(solution)/shard_map/concatenate | solution.py:140
  133.0 114.7 %gather_fusion = f32[32768,6]{1,0:T(8,128)} fusion(f32[32769,6]{1,0:T(8,128)} %concatenate.17, s32[32768]{0:T(1024)S(1)} %broadcast_clamp_fusion), kind=kCustom, calls=%fused_computation | custom fusion | bytes 1703936 | tf_op jit(solution)/shard_map/jit(_take)/gather | solution.py:141
  247.7 17.9 %select_bitcast_fusion = f32[6,32768]{0,1:T(8,128)S(1)} fusion(f32[32768,6]{1,0:T(8,128)} %gather_fusion, pred[32768]{0:T(1024)(128)(4,1)S(1)} %compare_and_fusion), kind=kLoop, calls=%fused_computation.114 | loop fusion | flops 196608 | bytes 1605632 | tf_op jit(solution)/shard_map/jit(_take)/select_n | solution.py:141
  265.7 13.2 %fusion.73 = (f32[3,32768]{0,1:T(8,128)}, f32[3,32768]{0,1:T(8,128)}) fusion(f32[6,32768]{0,1:T(8,128)S(1)} %select_bitcast_fusion), kind=kLoop, calls=%fused_computation.179 | loop fusion | bytes 1572864 | tf_op jit(solution)/shard_map/slice | solution.py:96
  281.4 9.7 %copy.143 = f32[3,256,128]{2,1,0:T(8,128)S(1)} copy(f32[3,256,128]{0,2,1:T(8,128)} %bitcast.253) | data formatting | bytes 786432 | tf_op jit(solution)/shard_map/while | solution.py:89
  291.1 10.4 %copy.146 = f32[3,256,128]{2,1,0:T(8,128)} copy(f32[3,256,128]{0,2,1:T(8,128)} %bitcast.252) | data formatting | bytes 786432 | tf_op jit(solution)/shard_map/while | solution.py:89
  301.5 79.0 %while.37 = (s32[]{:T(128)}, f32[16,3,16,56]{3,2,1,0:T(8,128)}, s32[16]{0:T(128)S(1)}, f32[3,256,128]{2,1,0:T(8,128)}, f32[3,256,56]{2,1,0:T(8,128)S(1)}, /*inde...) while((s32[]{:T(128)}, f32[16,3,16,56]{3,2,1,0:T(8,128)}, ...), condition=%wide.region_11.12_spmd, body=%wide.region_7.11_spmd.sunk | while | flops 3558023 | bytes 226507 | solution.py:89
  389.2 10.0 %copy.135 = f32[6,32768]{1,0:T(8,128)} copy(f32[6,32768]{0,1:T(8,128)} %copy-done.1) | data formatting | bytes 1572864 | tf_op jit(solution)/shard_map/jit(_take)/select_n | solution.py:141
  399.2 5.1 collective-permute-start
  407.9 15.4 %all-reduce.1 = f32[672]{0:T(1024)S(1)} all-reduce(f32[672]{0:T(1024)S(1)} %dynamic-update-slice), channel_id=2, replica_groups=mesh['gx_0'=4,'gx_1'=4,'gx_2'=8,'gy'=2] {'gx_0'}, use_global_device_ids=true, to_apply=%add.1 | all-reduce | flops 672 | bytes 5376
  423.4 9.1 all_gather.13
  432.5 18.4 %all_gather.14 = f32[128,1,168]{2,1,0:T(1,128)S(1)} all-gather(f32[16,1,168]{2,1,0:T(1,128)S(1)} %all_gather.13), channel_id=1, replica_groups=mesh['gx_0'=4,'gx_1'=4,'gx_2'=8,'gy'=2] {'gx_2'}, dimensions={0}, use_global_device_ids=true | all-gather | bytes 96768 | tf_op jit(solution)/shard_map/all_gather | solution.py:44
  451.0 23.6 %all_gather.15 = f32[256,1,168]{0,2,1:T(8,128)S(1)} all-gather(f32[128,1,168]{0,2,1:T(8,128)S(1)} %copy.155), channel_id=1, replica_groups=mesh['gx_0'=4,'gx_1'=4,'gx_2'=8,'gy'=2] {'gy'}, dimensions={0}, use_global_device_ids=true | all-gather | bytes 258048 | tf_op jit(solution)/shard_map/all_gather | solution.py:44
  481.9 9.0 gather_fusion.2
  495.9 8.1 fusion.60
  504.2 80.5 %while.38 = (s32[]{:T(128)}, f32[16,3,16,128]{3,2,1,0:T(8,128)S(1)}, s32[16]{0:T(128)S(1)}, f32[3,256,56]{2,1,0:T(8,128)S(1)}, f32[3,256,128]{2,1,0:T(8,128)}, /...) while((s32[]{:T(128)}, f32[16,3,16,128]{3,2,1,0:T(8,128)S(1)}, ...), condition=%wide.region_17.18_spmd, body=%wide.region_13.17_spmd.sunk | while | flops 3561479 | bytes 212175 | solution.py:89
  609.4 163.1 %while.36 = (s32[]{:T(128)}, f32[16,3,16,128]{3,2,1,0:T(8,128)S(1)}, s32[16]{0:T(128)S(1)}, f32[3,256,384]{2,1,0:T(8,128)}, f32[3,256,128]{2,1,0:T(8,128)}, /*in...) while((s32[]{:T(128)}, f32[16,3,16,128]{3,2,1,0:T(8,128)S(1)}, ...), condition=%wide.region_6.7_spmd, body=%wide.region_2.6_spmd.sunk | while | flops 24385544 | bytes 590031 | solution.py:89
  613.5 6.0 fusion.95
  623.7 6.0 fusion.95
  633.9 6.0 fusion.95
  644.1 6.0 fusion.95
  654.3 6.0 fusion.95
  664.5 6.0 fusion.95
  674.7 6.0 fusion.95
  684.9 6.0 fusion.95
  695.1 6.0 fusion.95
  705.3 6.0 fusion.95
  715.5 6.0 fusion.95
  725.7 6.0 fusion.95
  735.9 6.0 fusion.95
  746.1 6.0 fusion.95
  756.3 6.0 fusion.95
  766.4 6.0 fusion.95
  772.9 8.6 copy.162
  781.5 87.1 %scatter_custom_fusion.1 = f32[32769,3]{1,0:T(8,128)} fusion(s32[32768]{0:T(1024)} %bitcast.268, f32[32768,3]{1,0:T(8,128)} %copy.162, f32[]{:T(128)} %constant.196.clone.1), kind=kCustom, calls=%fused_computation.117 | custom fusion | bytes 393740 | tf_op jit(solution)/shard_map/scatter | solution.py:145
  868.6 11.2 %slice.217 = f32[32768,3]{1,0:T(8,128)} slice(f32[32769,3]{1,0:T(8,128)} %scatter_custom_fusion.1), slice={[0:32768], [0:3]} | slice | bytes 786432 | tf_op jit(solution)/shard_map/slice | solution.py:146
  879.8 9.9 %copy.163 = f32[3,128,256]{2,0,1:T(4,128)} copy(f32[3,128,256]{0,2,1:T(8,128)} %bitcast.251) | data formatting | bytes 786432 | tf_op jit(solution)/shard_map/reshape | solution.py:205
  889.7 7.4 all-to-all-start.1
  897.3 19.2 %all-to-all-done.1 = f32[3,128,256]{2,0,1:T(4,128)S(1)} async-done(((f32[3,128,256]{2,0,1:T(4,128)}), f32[3,128,256]{2,0,1:T(4,128)S(1)}, u32[]{:S(2)}, u32[]{:S(2)}) %all-to-all-start.1) | async-done | bytes 393248 | tf_op jit(solution)/shard_map/all_to_all | solution.py:204
  916.5 8.4 copy.164
  924.8 22.5 %gather_fusion.3 = f32[8704,3]{1,0:T(8,128)} fusion(f32[32768,3]{1,0:T(8,128)} %bitcast.248, s32[9216]{0:T(1024)S(1)} %pad_clamp_fusion), kind=kCustom, calls=%fused_computation.3 | custom fusion | bytes 243712 | tf_op jit(solution)/shard_map/jit(_take)/gather | solution.py:207
  947.4 7.8 select_bitcast_fusion.1
  (342 shorter events, 208.9 us)
Async XLA Ops:
  0.0 475.4 %copy-start = (f32[16,168,168]{2,1,0:T(8,128)S(1)}, f32[16,168,168]{2,1,0:T(8,128)}, u32[]{:S(2)}) copy-start(f32[16,168,168]{2,1,0:T(8,128)} %param.32) | copy-start | bytes 5419012
  53.2 27.7 %copy-start.14 = (s32[1,3,256]{2,0,1:T(1,128)S(1)}, s32[1,3,256]{2,0,1:T(1,128)}, u32[]{:S(2)}) copy-start(s32[1,3,256]{2,0,1:T(1,128)} %param.27) | copy-start | bytes 9220
  53.2 27.8 %copy-start.6 = (s32[1,32768]{1,0:T(1,128)S(1)}, s32[1,32768]{1,0:T(1,128)}, u32[]{:S(2)}) copy-start(s32[1,32768]{1,0:T(1,128)} %param.26) | copy-start | bytes 393220
  53.2 27.9 %copy-start.13 = (f32[3,1,256]{2,1,0:T(1,128)S(1)}, f32[3,1,256]{2,1,0:T(1,128)}, u32[]{:S(2)}) copy-start(f32[3,1,256]{2,1,0:T(1,128)} %param.25) | copy-start | bytes 9220
  53.3 28.0 %copy-start.12 = (s32[1,8,256]{2,1,0:T(8,128)S(1)}, s32[1,8,256]{2,1,0:T(8,128)}, u32[]{:S(2)}) copy-start(s32[1,8,256]{2,1,0:T(8,128)} %param.28) | copy-start | bytes 24580
  53.3 28.0 %copy-start.11 = (s32[1,8,256]{2,1,0:T(8,128)S(1)}, s32[1,8,256]{2,1,0:T(8,128)}, u32[]{:S(2)}) copy-start(s32[1,8,256]{2,1,0:T(8,128)} %param.29) | copy-start | bytes 24580
  63.4 46.9 %all-to-all-start = ((f32[6,128,256]{2,0,1:T(8,128)}), f32[6,128,256]{2,0,1:T(8,128)}, u32[]{:S(2)}, u32[]{:S(2)}) async-start(f32[6,128,256]{2,0,1:T(8,128)} %copy.133), calls=%async_computation | async-start | bytes 2097152 | tf_op jit(solution)/shard_map/all_to_all | solution.py:183
  81.2 38.5 %copy-start.7 = (s32[32768,1]{0,1:T(1,128)}, s32[32768,1]{0,1:T(1,128)S(1)}, u32[]{:S(2)}) copy-start(s32[32768,1]{0,1:T(1,128)S(1)} %compare_select_fusion) | copy-start | bytes 393220
  265.7 15.7 %copy-start.1 = (f32[6,32768]{0,1:T(8,128)}, f32[6,32768]{0,1:T(8,128)S(1)}, u32[]{:S(2)}) copy-start(f32[6,32768]{0,1:T(8,128)S(1)} %select_bitcast_fusion) | copy-start | bytes 2359300
  291.1 10.4 %copy-start.16 = (s32[16]{0:T(128)S(1)}, s32[16]{0:T(128)}, u32[]{:S(2)}) copy-start(s32[16]{0:T(128)} %iota_multiply_fusion) | copy-start | bytes 196
  380.5 0.7 copy-start.3
  380.5 7.3 copy-start.4
  384.6 94.1 %collective-permute-start.2 = (f32[168,256]{1,0:T(8,128)S(1)}, f32[168,256]{1,0:T(8,128)}, u32[]{:S(2)}, u32[]{:S(2)}) collective-permute-start(f32[168,256]{1,0:T(8,128)S(1)} %convolution_bitcast_fusion.1), channel_id=1, source_target_pairs={{0,2},{2,4},{4,6},{6,8},{8,10},{10,12},{12,14},{14,16},{16,18},{18... | collective-permute-start | bytes 516104 | tf_op jit(solution)/shard_map/ppermute | solution.py:29
  387.8 90.9 %collective-permute-start.3 = (f32[168,256]{1,0:T(8,128)S(1)}, f32[168,256]{1,0:T(8,128)}, u32[]{:S(2)}, u32[]{:S(2)}) collective-permute-start(f32[168,256]{1,0:T(8,128)S(1)} %convolution_bitcast_fusion.1), channel_id=1, source_target_pairs={{2,0},{4,2},{6,4},{8,6},{10,8},{12,10},{14,12},{16,14},{18,16},{20... | collective-permute-start | bytes 516104 | tf_op jit(solution)/shard_map/ppermute | solution.py:30
  399.2 75.9 %copy-start.15 = (s32[1,1,256]{2,1,0:T(1,128)S(1)}, s32[1,1,256]{2,1,0:T(1,128)}, u32[]{:S(2)}) copy-start(s32[1,1,256]{2,1,0:T(1,128)} %param.30) | copy-start | bytes 3076
  399.2 185.5 %collective-permute-start = (f32[6,32768]{1,0:T(8,128)}, f32[6,32768]{1,0:T(8,128)}, u32[]{:S(2)}, u32[]{:S(2)}) collective-permute-start(f32[6,32768]{1,0:T(8,128)} %copy.135), channel_id=1, source_target_pairs={{0,2},{2,4},{4,6},{6,8},{8,10},{10,12},{12,14},{14,16},{16,18},{18... | collective-permute-start | bytes 2359304 | tf_op jit(solution)/shard_map/ppermute | solution.py:29
  404.3 180.4 %collective-permute-start.1 = (f32[6,32768]{1,0:T(8,128)}, f32[6,32768]{1,0:T(8,128)}, u32[]{:S(2)}, u32[]{:S(2)}) collective-permute-start(f32[6,32768]{1,0:T(8,128)} %copy.135), channel_id=1, source_target_pairs={{2,0},{4,2},{6,4},{8,6},{10,8},{12,10},{14,12},{16,14},{18,16},{20... | collective-permute-start | bytes 2359304 | tf_op jit(solution)/shard_map/ppermute | solution.py:30
  475.1 1.5 copy-start.2
  490.8 5.1 copy-start.5
  588.6 4.8 copy-start.10
  879.8 17.3 %copy-start.9 = (s32[1,8704]{1,0:T(1,128)S(1)}, s32[1,8704]{1,0:T(1,128)}, u32[]{:S(2)}) copy-start(s32[1,8704]{1,0:T(1,128)} %param.24) | copy-start | bytes 104452
  879.8 17.4 %copy-start.8 = (s32[8704]{0:T(1024)S(1)}, s32[8704]{0:T(1024)}, u32[]{:S(2)}) copy-start(s32[8704]{0:T(1024)} %get-tuple-element.356) | copy-start | bytes 104452
  889.7 26.7 %all-to-all-start.1 = ((f32[3,128,256]{2,0,1:T(4,128)}), f32[3,128,256]{2,0,1:T(4,128)S(1)}, u32[]{:S(2)}, u32[]{:S(2)}) async-start(f32[3,128,256]{2,0,1:T(4,128)} %copy.163), calls=%async_computation.1 | async-start | bytes 1048576 | tf_op jit(solution)/shard_map/all_to_all | solution.py:204
where the time goes:
time: 978 us; the launch traced here: 959 us
  local copies, waits for them, and re-layouts  517 us (53%)
  other arithmetic  180 us (18%)
  loops' own time  90.5 us (9%)
  blocking collectives  66.5 us (7%)
  waiting for transfers between devices  44.2 us (5%)
  starting transfers between devices  35.3 us (4%)
  matrix products  23.9 us (2%)
    reduce_sum x48, other arithmetic, stokes_sum(): jnp.sum(push_x * direct + projected * delta_x, axis=2)  130 us
    scatter x2, local copies, waits for them, and re-layouts, place_rows(): jnp.zeros((length + 1, values.shape[0]), jnp.float32).at[where]  116 us
    gather x1, local copies, waits for them, and re-layouts, pick_slots(): return jnp.take(rows_view, table, axis=0).T  115 us
    another operation x3, loops' own time, by_blocks(): result = lax.map(one_block, starts)  90.5 us
    all_gather x3, blocking collectives, all_blocks(): tiles = lax.all_gather(tiles, axes[k], axis=0, tiled=True)  51.1 us
    mul x48, local copies, waits for them, and re-layouts, stokes_sum(): push_y * delta_y  38.7 us
    dynamic_slice x48, local copies, waits for them, and re-layouts, by_blocks(): result = lax.map(one_block, starts)  29 us
    while x4, local copies, waits for them, and re-layouts, by_blocks(): result = lax.map(one_block, starts)  25.4 us
  transfers between devices with their start and end apart: 6, of which 2 were waited for; matrix products, arithmetic and copies ran while one was open for 10% of the time, Pallas kernels for 0%

commit v1 on v0

v1 whole, which is shorter than its diff:
```python
import functools
import math

import jax
import jax.numpy as jnp
from jax import lax
from jax.experimental import pallas as pl
from jax.experimental.pallas import tpu as pltpu
from jax.sharding import PartitionSpec as P

P_SIZE = 544
NOPS = 16
TILE = 128
LANES = 128
SURF = 56
SURF_PAD = 64
SOFTENING = 0.25
RADIUS = 2.5
HIGHEST = lax.Precision.HIGHEST
F32 = jnp.float32
BF16 = jnp.bfloat16

VMEM = pl.BlockSpec(memory_space=pltpu.VMEM)
SMEM = pl.BlockSpec(memory_space=pltpu.SMEM)


def params():
    return pltpu.CompilerParams(vmem_limit_bytes=60 * 1024 * 1024)


def sphere_points(count):
    index = jnp.arange(count).astype(F32)
    height = 1.0 - (2.0 * index + 1.0) / count
    radial = jnp.sqrt(1.0 - height * height)
    angle = 2.399963 * index
    return jnp.stack([radial * jnp.cos(angle), radial * jnp.sin(angle), height])


def aligned(index, step):
    return pl.multiple_of(index * step, step)


def split_bf16(value):
    high = value.astype(BF16)
    low = (value - high.astype(F32)).astype(BF16)
    return high, low


def dot_nt(left, right):
    return lax.dot_general(left, right, (((1,), (1,)), ((), ())), preferred_element_type=F32)


def dot_nn(left, right):
    return lax.dot_general(left, right, (((1,), (0,)), ((), ())), preferred_element_type=F32)


def move_rows(write, indices, block):
    part = indices.at[pl.ds(block * TILE, TILE)]
    for row in range(TILE):
        write(row, part[row])


def to_rows_table(source, table, blocks, width):
    def one(block, carry):
        rows = source[pl.ds(block * width, width), :]
        table[pl.ds(aligned(block, TILE), TILE), 0:width] = rows.T
        return carry

    lax.fori_loop(0, blocks, one, 0, unroll=4)


def from_rows_table(table, out, blocks, width):
    def one(block, carry):
        rows = table[pl.ds(aligned(block, TILE), TILE), 0:8].T
        out[pl.ds(block * width, width), :] = rows[0:width]
        return carry

    lax.fori_loop(0, blocks, one, 0, unroll=4)


def send_kernel(dest, packed, out, table, stage):
    blocks = packed.shape[1] // LANES

    def one(block, carry):
        stage[:, 0:8] = packed[:, pl.ds(aligned(block, LANES), LANES)].T

        def write(row, index):
            table[pl.ds(index, 1), :] = stage[pl.ds(row, 1), :]

        move_rows(write, dest, block)
        return carry

    lax.fori_loop(0, blocks, one, 0)
    from_rows_table(table, out, out.shape[0] // 6, 6)


def features(x_rows, g_rows, store_a, store_d):
    gdotx = g_rows[0] * x_rows[0] + g_rows[1] * x_rows[1] + g_rows[2] * x_rows[2]
    for c in range(3):
        store_d(c, g_rows[c])
        store_a(c, gdotx * x_rows[c])
    for k in range(3):
        for c in range(3):
            store_a(3 + 3 * k + c, g_rows[k] * x_rows[c])
    for k in range(3):
        store_a(12 + k, g_rows[k])
    store_a(15, gdotx)


def combine(sums, y_rows):
    along = (
        y_rows[0] * sums[12:13] + y_rows[1] * sums[13:14] + y_rows[2] * sums[14:15] - sums[15:16]
    )
    flows = []
    for c in range(3):
        crossed = y_rows[0] * sums[3 + c : 4 + c]
        crossed = crossed + y_rows[1] * sums[6 + c : 7 + c]
        crossed = crossed + y_rows[2] * sums[9 + c : 10 + c]
        flows.append(sums[c : c + 1] + y_rows[c] * along - crossed)
    return flows


def pair_weights(dx, dy, dz):
    soft_sq = (dx * dx + dy * dy) + (dz * dz + SOFTENING)
    root = lax.rsqrt(soft_sq)
    cube = root * root * root
    return cube, root + SOFTENING * cube


def receive_kernel(source, centers, arrived, surface, surf_rows, tiles, checks, table, stage, feat):
    leaves = tiles.shape[0] // 6
    slots = leaves * TILE
    to_rows_table(arrived, table, slots // TILE, 6)
    table[pl.ds(slots, 8), :] = jnp.zeros((8, LANES), F32)
    feat[...] = jnp.zeros(feat.shape, F32)

    def gather(leaf, slot):
        def write(row, index):
            stage[pl.ds(slot * TILE + row, 1), :] = table[pl.ds(index, 1), :]

        move_rows(write, source, leaf)

    def check(leaf, slot):
        rows = stage[slot * TILE : slot * TILE + TILE, 0:8].T
        tiles[pl.ds(leaf * 6, 6), :] = rows[0:6]
        x_rows = [rows[c : c + 1] - centers[c * leaves + leaf] for c in range(3)]
        g_rows = [rows[3 + c : 4 + c] for c in range(3)]

        def store_a(row, value):
            feat[slot * 32 + row : slot * 32 + row + 1, :] = value

        def store_d(row, value):
            feat[slot * 32 + 16 + row : slot * 32 + 17 + row, :] = value

        features(x_rows, g_rows, store_a, store_d)
        both = feat[slot * 32 : slot * 32 + 32, :]
        high, low = split_bf16(both)
        cube, direct = pair_weights(
            surface[0] - x_rows[0], surface[1] - x_rows[1], surface[2] - x_rows[2]
        )
        cube_high, cube_low = split_bf16(cube)
        dir_high, dir_low = split_bf16(direct)
        sums = dot_nt(high[0:16], cube_high) + dot_nt(high[0:16], cube_low)
        sums = sums + dot_nt(low[0:16], cube_high) + dot_nt(high[16:32], dir_high)
        sums = sums + dot_nt(high[16:32], dir_low) + dot_nt(low[16:32], dir_high)
        flows = combine(sums, [surf_rows[c : c + 1, 0:SURF_PAD] for c in range(3)])
        for c in range(3):
            checks[pl.ds(leaf * 3 + c, 1), 0:SURF_PAD] = flows[c]

    gather(0, 0)

    def pair(step, carry):
        leaf = step * 2
        gather(leaf + 1, 1)
        check(leaf, 0)
        gather(jnp.minimum(leaf + 2, leaves - 1), 0)
        check(leaf + 1, 1)
        return carry

    lax.fori_loop(0, leaves // 2, pair, 0)


def near_kernel(listed, places, centers, own, extended, *rest):
    before = rest[0] if len(rest) == 3 else None
    out, target = rest[-2:]
    leaves = own.shape[0] // 6

    def one(leaf, carry):
        shift = [centers[c * leaves + leaf] for c in range(3)]
        rows = own[pl.ds(leaf * 6, 6), :]
        target[:, 0:6] = rows.T
        y_rows = [own[pl.ds(leaf * 6 + c, 1), :] - shift[c] for c in range(3)]
        left_d, left_w, sources = [], [], []
        for n in range(listed):
            place = places[n * leaves + leaf] * 6
            tile = [extended[pl.ds(place + c, 1), :] for c in range(6)]
            sources.append([jnp.broadcast_to(row, (8, LANES)) for row in tile])
            grow = [split_bf16(tile[3 + c]) for c in range(3)]
            xrow = [split_bf16(tile[c] - shift[c]) for c in range(3)]
            ones = jnp.ones((1, LANES), BF16)
            zero = jnp.zeros((1, LANES), BF16)
            left_d.append(jnp.concatenate([g[0] for g in grow] + [g[1] for g in grow] + [zero] * 10))
            left_w.append(
                jnp.concatenate([x[0] for x in xrow] + [x[1] for x in xrow] + [ones] + [zero] * 9)
            )
        sum_d = jnp.zeros((16, TILE), F32)
        sum_w = jnp.zeros((16, TILE), F32)
        sum_dl = jnp.zeros((16, TILE), F32)
        sum_wl = jnp.zeros((16, TILE), F32)
        directs = [[] for _ in range(listed)]
        pushes = [[] for _ in range(listed)]
        for block in range(TILE // 8):
            y = [
                jnp.broadcast_to(target[8 * block : 8 * block + 8, c : c + 1], (8, LANES))
                for c in range(3)
            ]
            for n in range(listed):
                x = sources[n]
                dx, dy, dz = y[0] - x[0], y[1] - x[1], y[2] - x[2]
                cube, direct = pair_weights(dx, dy, dz)
                directs[n].append(direct)
                pushes[n].append(cube * ((x[3] * dx + x[4] * dy) + x[5] * dz))
        for n in range(listed):
            dir_high, dir_low = split_bf16(jnp.concatenate(directs[n]))
            push_high, push_low = split_bf16(jnp.concatenate(pushes[n]))
            sum_d = sum_d + dot_nt(left_d[n], dir_high)
            sum_dl = sum_dl + dot_nt(left_d[n], dir_low)
            sum_w = sum_w + dot_nt(left_w[n], push_high)
            sum_wl = sum_wl + dot_nt(left_w[n], push_low)
        whole = sum_w[6:7] + sum_wl[6:7]
        for c in range(3):
            direct = sum_d[c : c + 1] + sum_d[3 + c : 4 + c] + sum_dl[c : c + 1]
            moved = sum_w[c : c + 1] + sum_w[3 + c : 4 + c] + sum_wl[c : c + 1]
            total = direct + (y_rows[c] * whole - moved)
            if before is not None:
                total = total + before[pl.ds(leaf * 3 + c, 1), :]
            out[pl.ds(leaf * 3 + c, 1), :] = total
        return carry

    lax.fori_loop(0, leaves, one, 0)


def far_kernel(source, centers, own, near, local, surface, surf_rows, out, table, stage, feat):
    leaves = own.shape[0] // 6
    scale = 1.0 / (8.0 * math.pi)
    feat[...] = jnp.zeros(feat.shape, F32)
    stage[...] = jnp.zeros(stage.shape, F32)

    def scatter(leaf, slot):
        def write(row, index):
            table[pl.ds(index, 1), :] = stage[pl.ds(slot * TILE + row, 1), :]

        move_rows(write, source, leaf)

    def far(leaf, slot):
        y_rows = [own[pl.ds(leaf * 6 + c, 1), :] - centers[c * leaves + leaf] for c in range(3)]
        g_rows = [local[pl.ds(leaf * 3 + c, 1), :] for c in range(3)]
        x_rows = [surf_rows[c : c + 1, :] for c in range(3)]

        def store_a(row, value):
            feat[slot * 32 + row : slot * 32 + row + 1, :] = value

        def store_d(row, value):
            feat[slot * 32 + 16 + row : slot * 32 + 17 + row, :] = value

        features(x_rows, g_rows, store_a, store_d)
        both = feat[slot * 32 : slot * 32 + 32, 0:SURF_PAD]
        high, low = split_bf16(both)
        cube, direct = pair_weights(
            y_rows[0] - surface[0], y_rows[1] - surface[1], y_rows[2] - surface[2]
        )
        cube_high, cube_low = split_bf16(cube)
        dir_high, dir_low = split_bf16(direct)
        sums = dot_nn(high[0:16], cube_high) + dot_nn(high[0:16], cube_low)
        sums = sums + dot_nn(low[0:16], cube_high) + dot_nn(high[16:32], dir_high)
        sums = sums + dot_nn(high[16:32], dir_low) + dot_nn(low[16:32], dir_high)
        flows = combine(sums, y_rows)
        total = [(flows[c] + near[pl.ds(leaf * 3 + c, 1), :]) * scale for c in range(3)]
        for c in range(3):
            feat[64 + slot * 8 + c : 65 + slot * 8 + c, :] = total[c]
        stage[slot * TILE : slot * TILE + TILE, 0:8] = feat[64 + slot * 8 : 72 + slot * 8, :].T

    far(0, 0)

    def pair(step, carry):
        leaf = step * 2
        far(leaf + 1, 1)
        scatter(leaf, 0)
        far(jnp.minimum(leaf + 2, leaves - 1), 0)
        scatter(leaf + 1, 1)
        return carry

    lax.fori_loop(0, leaves // 2, pair, 0)
    from_rows_table(table, out, out.shape[0] // 3, 3)


def return_kernel(dest, arrived, out, table, stage):
    to_rows_table(arrived, table, arrived.shape[0] // 3, 3)

    def one(block, carry):
        def write(row, index):
            stage[pl.ds(row, 1), :] = table[pl.ds(index, 1), :]

        move_rows(write, dest, block)
        out[:, pl.ds(aligned(block, LANES), LANES)] = stage[:, 0:8].T
        return carry

    lax.fori_loop(0, out.shape[1] // LANES, one, 0)


def exchange(rows, owners):
    blocks = rows.reshape(owners, 1, -1)
    blocks = lax.all_to_all(blocks, "gx", split_axis=0, concat_axis=0, tiled=True)
    return blocks.reshape(rows.shape)


def near_sum(listed, places, centers, tiles, extended, before):
    return pl.pallas_call(
        functools.partial(near_kernel, listed),
        out_shape=jax.ShapeDtypeStruct((tiles.shape[0] // 2, LANES), F32),
        in_specs=[SMEM, SMEM, VMEM, VMEM] + [VMEM] * len(before),
        out_specs=VMEM,
        scratch_shapes=[pltpu.VMEM((TILE, LANES), F32)],
        compiler_params=params(),
        cost_estimate=pl.CostEstimate(
            flops=listed * 10**10, transcendentals=0, bytes_accessed=10**7
        ),
        name=f"near{listed}",
    )(places, centers, tiles, extended, *before)


def halo(shard, devices):
    up = [(i, i + 1) for i in range(devices - 1)]
    down = [(i + 1, i) for i in range(devices - 1)]
    before = lax.ppermute(shard, "gx", up)
    after = lax.ppermute(shard, "gx", down)
    return jnp.concatenate([before, shard, after], axis=0)


def body(
    positions,
    forces,
    deriv_mat,
    quad_mat,
    point_dest,
    leaf_center,
    tile_src,
    neighbours,
    inter_leaf,
    inter_op,
    coarse_op,
    up_pinv,
    trans_ops,
    child_ops,
):
    owners = lax.axis_size("gx")
    count = positions.shape[2]
    leaves = leaf_center.shape[2]
    slots = leaves * TILE
    expansion = up_pinv.shape[0]
    shape = jax.ShapeDtypeStruct
    first = lax.axis_index("gx") * leaves - leaves

    tangent = jnp.dot(
        positions.reshape(-1, P_SIZE), deriv_mat, precision=HIGHEST, preferred_element_type=F32
    ).reshape(3, count)
    jacobian = jnp.sqrt(1.0 + jnp.sum(tangent * tangent, axis=0))
    weighted = jnp.dot(
        forces.reshape(-1, P_SIZE), quad_mat, precision=HIGHEST, preferred_element_type=F32
    ).reshape(3, count)
    packed = jnp.concatenate(
        [positions.reshape(3, count), weighted * jacobian[None], jnp.zeros((2, count), F32)], axis=0
    )
    outgoing = pl.pallas_call(
        send_kernel,
        out_shape=shape((6 * slots // LANES, LANES), F32),
        in_specs=[SMEM, VMEM],
        out_specs=VMEM,
        scratch_shapes=[pltpu.VMEM((slots, LANES), F32), pltpu.VMEM((TILE, LANES), F32)],
        compiler_params=params(),
        name="send",
    )(point_dest.reshape(count), packed)
    arrived = exchange(outgoing, owners)

    source = tile_src.reshape(slots)
    centers = leaf_center.reshape(3 * leaves)
    sphere = RADIUS * sphere_points(SURF)
    surf_rows = jnp.pad(sphere, ((0, 5), (0, LANES - SURF)))
    surface = jnp.broadcast_to(surf_rows[:3, :SURF_PAD, None], (3, SURF_PAD, LANES))
    tiles, checks = pl.pallas_call(
        receive_kernel,
        out_shape=[shape((6 * leaves, LANES), F32), shape((3 * leaves, LANES), F32)],
        in_specs=[SMEM, SMEM, VMEM, VMEM, VMEM],
        out_specs=[VMEM, VMEM],
        scratch_shapes=[
            pltpu.VMEM((slots + 8, LANES), F32),
            pltpu.VMEM((2 * TILE, LANES), F32),
            pltpu.VMEM((64, LANES), F32),
        ],
        compiler_params=params(),
        name="receive",
    )(source, centers, arrived, surface, surf_rows)

    extended = halo(tiles, owners)
    check = checks.reshape(leaves, 3, LANES)[:, :, :SURF].reshape(leaves, expansion)
    multipole = jnp.dot(check, up_pinv, precision=HIGHEST, preferred_element_type=F32)
    multipole_ext = halo(multipole, owners)
    grouped = jnp.sum(multipole.reshape(leaves // 8, 8, expansion), axis=0)
    moment = jnp.einsum("ce,cef->f", grouped, child_ops, precision=HIGHEST)
    moment = jnp.pad(moment, (0, 8 * LANES - expansion)).reshape(8, LANES)
    coarse = lax.all_gather(moment, ("gx", "gy"), axis=0, tiled=True)

    near = near_sum(1, jnp.arange(leaves), centers, tiles, tiles, [])
    places = (neighbours[0, 1:] - first).reshape(2 * leaves)
    near = near_sum(2, places, centers, tiles, extended, [near])

    near, coarse, multipole_ext = lax.optimization_barrier((near, coarse, multipole_ext))
    coarse = coarse.reshape(-1, 8, LANES)[:, :2].reshape(-1, 2 * LANES)[:, :expansion]
    op_ids = jnp.arange(NOPS)
    onehot = (coarse_op[0, 0][:, None] == op_ids[None, :]).astype(F32)
    by_op = jnp.einsum("bk,be->ke", onehot, coarse, precision=HIGHEST)
    coarse_local = jnp.einsum("ke,kef->f", by_op, trans_ops, precision=HIGHEST)
    pushed = jnp.einsum("cfe,e->cf", child_ops, coarse_local, precision=HIGHEST)

    picked = jnp.take(multipole_ext, (inter_leaf[0] - first).T, axis=0)
    leaf_hot = (inter_op[0].T[:, :, None] == op_ids[None, None, :]).astype(F32)
    leaf_by_op = jnp.einsum("nje,njk->nke", picked, leaf_hot, precision=HIGHEST)
    local = jnp.dot(
        leaf_by_op.reshape(leaves, NOPS * expansion),
        trans_ops.reshape(NOPS * expansion, expansion),
        precision=HIGHEST,
        preferred_element_type=F32,
    )
    local = (local.reshape(leaves // 8, 8, expansion) + pushed[None]).reshape(leaves, 3, SURF)
    local = jnp.pad(local, ((0, 0), (0, 0), (0, LANES - SURF))).reshape(3 * leaves, LANES)

    returning = pl.pallas_call(
        far_kernel,
        out_shape=shape((3 * slots // LANES, LANES), F32),
        in_specs=[SMEM, SMEM, VMEM, VMEM, VMEM, VMEM, VMEM],
        out_specs=VMEM,
        scratch_shapes=[
            pltpu.VMEM((slots + 8, LANES), F32),
            pltpu.VMEM((2 * TILE, LANES), F32),
            pltpu.VMEM((80, LANES), F32),
        ],
        compiler_params=params(),
        name="far",
    )(source, centers, tiles, near, local, surface, surf_rows)
    came_back = exchange(returning, owners)
    velocity = pl.pallas_call(
        return_kernel,
        out_shape=shape((8, count), F32),
        in_specs=[SMEM, VMEM],
        out_specs=VMEM,
        scratch_shapes=[pltpu.VMEM((slots, LANES), F32), pltpu.VMEM((TILE, LANES), F32)],
        compiler_params=params(),
        name="back",
    )(point_dest.reshape(count), came_back)
    return velocity[:3].reshape(3, 1, count)


def solution(mesh):
    in_specs = (
        P(None, "gy", "gx"),
        P(None, "gy", "gx"),
        P(),
        P(),
        P("gy", "gx"),
        P(None, "gy", "gx"),
        P("gy", "gx"),
        P("gy", None, "gx"),
        P("gy", None, "gx"),
        P("gy", None, "gx"),
        P("gy", "gx", None),
        P(),
        P(),
        P(),
    )
    out_specs = P(None, "gy", "gx")
    return jax.shard_map(body, mesh=mesh, in_specs=in_specs, out_specs=out_specs, check_vma=False)
```

time: 978 us -> 573 us (0.59); the launches traced: 959 us -> 570 us
  local copies, waits for them, and re-layouts: 517 us -> 34.4 us
  Pallas kernels: 0 us -> 422 us
  other arithmetic: 180 us -> 10.1 us
  loops' own time: 90.5 us -> 0 us
  blocking collectives: 66.5 us -> 25.8 us
  waiting for transfers between devices: 44.2 us -> 15.6 us
  between operations: 1.35 us -> 13.6 us
    pallas_call x0 -> x6, Pallas kernels: none -> 422 us  [the longest x2 243 us: near_sum(): pl.pallas_call(functools.partial(near_kernel, listed), out_shape=jax.Shap...]
    gather x4 -> x1, local copies, waits for them, and re-layouts: 151 us -> 8.57 us  [body(): picked = jnp.take(multipole_ext, (inter_leaf[0] - first).T, axis=0)]
    reduce_sum x49 -> x1, other arithmetic: 130 us -> 0.04 us  [body(): grouped = jnp.sum(multipole.reshape(leaves // 8, 8, expansion), axis=0)]
    scatter x2 -> x0, local copies, waits for them, and re-layouts: 116 us -> none  [place_rows(): jnp.zeros((length + 1, values.shape[0]), jnp.float32).at[where]]
    another operation x3 -> x0, loops' own time: 90.5 us -> none  [by_blocks(): result = lax.map(one_block, starts)]
    all_gather x3 -> x0, blocking collectives: 51.1 us -> none  [all_blocks(): tiles = lax.all_gather(tiles, axes[k], axis=0, tiled=True)]
    slice x6 -> x3, local copies, waits for them, and re-layouts: 42.8 us -> 2.84 us  [the longest x1 1.4 us: body(): coarse.reshape(-1, 8, LANES)[:, :2].reshape(-1, 2 * LANES)[:, :expansion]]
    mul x48 -> x0, local copies, waits for them, and re-layouts: 38.7 us -> none  [stokes_sum(): push_y * delta_y]
  transfers between devices with their start and end apart: 6 -> 6, of which waited for: 2 -> 1; matrix products, arithmetic and copies ran while one was open for 10% -> 3% of each run, Pallas kernels for 0% -> 43%
where the time goes in v1:
time: 573 us; the launch traced here: 570 us
  Pallas kernels  422 us (74%)
  local copies, waits for them, and re-layouts  34.4 us (6%)
  starting transfers between devices  27.8 us (5%)
  blocking collectives  25.8 us (5%)
  matrix products  20.9 us (4%)
  waiting for transfers between devices  15.6 us (3%)
  between operations  13.6 us (2%)
  other arithmetic  10.1 us (2%)
    pallas_call x2, Pallas kernels, near_sum(): pl.pallas_call(functools.partial(near_kernel, listed), out_shape=jax.Shap...  243 us
    pallas_call x1, Pallas kernels, body(): pl.pallas_call(receive_kernel, out_shape=[shape((6 * leaves, LANES), F32)...  74.6 us
    pallas_call x1, Pallas kernels, body(): pl.pallas_call(far_kernel, out_shape=shape((3 * slots // LANES, LANES), F...  62.4 us
    all_to_all x1, blocking collectives, exchange(): lax.all_to_all(blocks, 'gx', split_axis=0, concat_axis=0, tiled=True)  25.8 us
    pallas_call x1, Pallas kernels, body(): pl.pallas_call(return_kernel, out_shape=shape((8, count), F32), in_specs=...  21.8 us
    pallas_call x1, Pallas kernels, body(): pl.pallas_call(send_kernel, out_shape=shape((6 * slots // LANES, LANES),...  20.4 us
    all_to_all x1, starting transfers between devices, exchange(): lax.all_to_all(blocks, 'gx', split_axis=0, concat_axis=0, tiled=True)  16.3 us
    all_to_all x1, waiting for transfers between devices, exchange(): lax.all_to_all(blocks, 'gx', split_axis=0, concat_axis=0, tiled=True)  15.6 us
  transfers between devices with their start and end apart: 6, of which 1 were waited for; matrix products, arithmetic and copies ran while one was open for 3% of the time, Pallas kernels for 43%

profile of v1, /device:TPU:1, one launch (start us, length us, event | category | flops | bytes accessed | tf_op | source)
XLA Modules:
  0.0 570.2 jit_solution(7063643259438419947)
XLA Ops:
  6.5 1.1 copy.53
  7.6 1.2 reduce.3
  8.8 1.2 reduce.2
  10.1 2.3 fusion.10
  12.7 2.3 convolution_multiply_fusion
  15.3 0.7 reduce.dest
  16.1 0.8 maximum_maximum_fusion.packed
  16.9 20.4 %send.1 = f32[1536,128]{1,0:T(8,128)} custom-call(s32[8704]{0:T(1024)} %reduce.dest, f32[8,8704]{1,0:T(8,128)} %maximum_maximum_fusion.packed), custom_call_target="tpu_custom_call" | custom-call | tf_op jit(solution)/shard_map/send/pallas_call | solution.py:374
  37.2 16.3 %all-to-all-start = ((f32[128,1,1536]{2,1,0:T(1,128)}), f32[128,1,1536]{2,1,0:T(1,128)S(1)}, u32[]{:S(2)}, u32[]{:S(2)}) async-start(f32[128,1,1536]{2,1,0:T(1,128)} %bitcast.62), calls=%async_computation | async-start | bytes 1572864 | tf_op jit(solution)/shard_map/all_to_all | solution.py:313
  54.3 0.6 pad.12.surf_rows
  54.9 0.6 reshape.136.centers
  55.5 0.7 compare_and_fusion
  56.2 0.7 copy.32
  57.0 0.8 copy.33
  57.7 1.0 reshape.157
  58.8 1.5 copy.31
  60.2 1.3 pad_slice_fusion
  61.5 1.2 slice_subtract_fusion
  62.7 15.6 %all-to-all-done = f32[128,1,1536]{2,1,0:T(1,128)S(1)} async-done(((f32[128,1,1536]{2,1,0:T(1,128)}), f32[128,1,1536]{2,1,0:T(1,128)S(1)}, u32[]{:S(2)}, u32[]{:S(2)}) %all-to-all-start) | async-done | bytes 786464 | tf_op jit(solution)/shard_map/all_to_all | solution.py:313
  78.3 1.4 broadcast_in_dim.27.surface
  79.7 74.6 %receive.1 = (f32[1536,128]{1,0:T(8,128)}, f32[768,128]{1,0:T(8,128)}) custom-call(s32[32768]{0:T(1024)} %bitcast.70, f32[768]{0:T(1024)} %reshape.136.centers, f32[1536,128]{1,0:T(8,128)} %bitcast.61, f32[3,64,128]{2,1,0:T(8,128)} %broadcast_in_dim.27.surface, f32[8,128]{1,0:T(8,128)} %pad.12.surf_rows), custom_call_target="tpu_custom_call" | custom-call | tf_op jit(solution)/shard_map/receive/pallas_call | solution.py:390
  154.3 1.2 reshape.143
  155.6 1.4 fusion.11
  157.1 1.3 collective-permute-start.3
  158.4 4.0 collective-permute-start.2
  162.5 1.3 collective-permute-start.1
  163.8 4.9 collective-permute-start
  168.7 2.0 fusion.7
  170.8 0.6 pad_bitcast_fusion
  172.0 112.2 %near1.1.rest_0_ = f32[768,128]{1,0:T(8,128)} custom-call(s32[256]{0:T(256)} %iota.21.places, f32[768]{0:T(1024)} %reshape.136.centers, f32[1536,128]{1,0:T(8,128)} %get-tuple-element.10.own.extended, f32[1536,128]{1,0:T(8,128)} %get-tuple-element.10.own.extended), custom_call_target="tpu_custom_call" | custom-call | flops 10000000000 | bytes 10000000 | tf_op jit(solution)/shard_map/near1/pallas_call | solution.py:318
  284.2 0.8 pad_maximum_fusion.1
  285.0 3.2 pad_maximum_fusion.extended
  288.2 130.5 %near2.1.near = f32[768,128]{1,0:T(8,128)} custom-call(s32[512]{0:T(512)} %bitcast.77, f32[768]{0:T(1024)} %reshape.136.centers, f32[1536,128]{1,0:T(8,128)} %get-tuple-element.10.own.extended, f32[4608,128]{1,0:T(8,128)} %pad_maximum_fusion.extended, f32[768,128]{1,0:T(8,128)} %near1.1.rest_0_), custom_call_target="tpu_custom_call" | custom-call | flops 20000000000 | bytes 10000000 | tf_op jit(solution)/shard_map/near2/pallas_call | solution.py:318
  418.7 1.4 slice.27
  420.5 1.3 convolution_bitcast_fusion.1
  421.8 1.2 fusion.12
  423.0 1.3 copy.34
  424.4 8.6 %gather_fusion = f32[2048,168]{1,0:T(8,128)} fusion(f32[768,168]{1,0:T(8,128)S(1)} %copy.34, s32[2048]{0:T(1024)S(1)} %broadcast_clamp_fusion), kind=kCustom, calls=%fused_computation | custom fusion | bytes 2760704 | tf_op jit(solution)/shard_map/jit(_take)/gather | solution.py:425
  432.9 5.9 %fusion = f32[256,16,168]{2,1,0:T(8,128)} fusion(f32[2048,168]{1,0:T(8,128)} %gather_fusion, pred[256,8]{1,0:T(8,128)(4,1)} %copy.32, s32[256,8]{1,0:T(8,128)} %copy.31), kind=kOutput, calls=%fused_computation.3 | convolution fusion | flops 66437120 | bytes 4139008 | tf_op jit(solution)/shard_map/nje,njk->nke/dot_general | solution.py:427
  438.8 5.4 dot_general.34
  444.2 4.3 convolution_add_fusion
  448.8 0.9 pad.14
  449.6 2.0 reshape.151.local
  451.6 62.4 %far.1 = f32[768,128]{1,0:T(8,128)} custom-call(s32[32768]{0:T(1024)} %bitcast.71, f32[768]{0:T(1024)} %reshape.136.centers, f32[1536,128]{1,0:T(8,128)} %get-tuple-element.10.own.extended, f32[768,128]{1,0:T(8,128)} %near2.1.near, f32[768,128]{1,0:T(8,128)} %reshape.151.local, f32[3,64,128]{2,1,0:T(8,128)} %broadcast_in_dim.27.surface, f32[8,128]{1,0:T(8,128)} %pad.12.surf_rows), custom_call_target="tpu_custom_call" | custom-call | tf_op jit(solution)/shard_map/far/pallas_call | solution.py:437
  513.9 25.8 %all_to_all.10 = f32[128,1,768]{2,1,0:T(1,128)} all-to-all(f32[128,1,768]{2,1,0:T(1,128)} %bitcast.65), channel_id=1, replica_groups=mesh['gx'=128,'gy'=2] {'gx'}, dimensions={0} | all-to-all | bytes 786432 | tf_op jit(solution)/shard_map/all_to_all | solution.py:313
  539.8 21.8 %back.1 = f32[8,8704]{1,0:T(8,128)} custom-call(s32[8704]{0:T(1024)} %reduce.dest, f32[768,128]{1,0:T(8,128)} %bitcast.64), custom_call_target="tpu_custom_call" | custom-call | tf_op jit(solution)/shard_map/back/pallas_call | solution.py:451
  561.6 1.0 slice_bitcast_fusion
  562.6 0.8 copy.37
  (43 shorter events, 3.1 us)
Async XLA Ops:
  6.5 414.0 %copy-start = (f32[16,168,168]{2,1,0:T(8,128)S(1)}, f32[16,168,168]{2,1,0:T(8,128)}, u32[]{:S(2)}) copy-start(f32[16,168,168]{2,1,0:T(8,128)} %param.26) | copy-start | bytes 5419012
  10.1 5.2 copy-start.3
  15.0 39.9 %copy-start.5 = (f32[3,1,256]{2,1,0:T(1,128)S(1)}, f32[3,1,256]{2,1,0:T(1,128)}, u32[]{:S(2)}) copy-start(f32[3,1,256]{2,1,0:T(1,128)} %param.19) | copy-start | bytes 9220
  37.2 41.1 %all-to-all-start = ((f32[128,1,1536]{2,1,0:T(1,128)}), f32[128,1,1536]{2,1,0:T(1,128)S(1)}, u32[]{:S(2)}, u32[]{:S(2)}) async-start(f32[128,1,1536]{2,1,0:T(1,128)} %bitcast.62), calls=%async_computation | async-start | bytes 1572864 | tf_op jit(solution)/shard_map/all_to_all | solution.py:313
  53.6 365.2 %all-gather.2.cloned.1.call-start = ((), (), s32[]{:S(2)}) async-start(), calls=%async_computation.2 | async-start | bytes 1052672 | tf_op jit(solution)/shard_map/all_gather | solution.py:411
  53.7 0.6 copy-start.4
  78.3 1.4 copy-start.2
  157.1 127.1 %collective-permute-start.3 = (f32[256,168]{0,1:T(8,128)S(1)}, f32[256,168]{0,1:T(8,128)S(1)}, u32[]{:S(2)}, u32[]{:S(2)}) collective-permute-start(f32[256,168]{0,1:T(8,128)S(1)} %fusion.11), channel_id=1, source_target_pairs={{2,0},{4,2},{6,4},{8,6},{10,8},{12,10},{14,12},{16,14},{18,16},{20... | collective-permute-start | bytes 516104 | tf_op jit(solution)/shard_map/ppermute | solution.py:336
  158.4 125.8 %collective-permute-start.2 = (f32[256,168]{0,1:T(8,128)S(1)}, f32[256,168]{0,1:T(8,128)S(1)}, u32[]{:S(2)}, u32[]{:S(2)}) collective-permute-start(f32[256,168]{0,1:T(8,128)S(1)} %fusion.11), channel_id=1, source_target_pairs={{0,2},{2,4},{4,6},{6,8},{8,10},{10,12},{12,14},{14,16},{16,18},{18... | collective-permute-start | bytes 516104 | tf_op jit(solution)/shard_map/ppermute | solution.py:335
  162.5 122.6 %collective-permute-start.1 = (f32[1536,128]{1,0:T(8,128)}, f32[1536,128]{1,0:T(8,128)}, u32[]{:S(2)}, u32[]{:S(2)}) collective-permute-start(f32[1536,128]{1,0:T(8,128)} %get-tuple-element.10.own.extended), channel_id=1, source_target_pairs={{2,0},{4,2},{6,4},{8,6},{10,8},{12,10},{14,12},{16,14},{18,16},{20... | collective-permute-start | bytes 2359304 | tf_op jit(solution)/shard_map/ppermute | solution.py:336
  163.8 121.3 %collective-permute-start = (f32[1536,128]{1,0:T(8,128)}, f32[1536,128]{1,0:T(8,128)}, u32[]{:S(2)}, u32[]{:S(2)}) collective-permute-start(f32[1536,128]{1,0:T(8,128)} %get-tuple-element.10.own.extended), channel_id=1, source_target_pairs={{0,2},{2,4},{4,6},{6,8},{8,10},{10,12},{12,14},{14,16},{16,18},{18... | collective-permute-start | bytes 2359304 | tf_op jit(solution)/shard_map/ppermute | solution.py:335
  288.2 132.0 %copy-start.6 = (s32[1,1,256]{2,1,0:T(1,128)S(1)}, s32[1,1,256]{2,1,0:T(1,128)}, u32[]{:S(2)}) copy-start(s32[1,1,256]{2,1,0:T(1,128)} %param.24) | copy-start | bytes 3076
  418.7 3.0 copy-start.1
Sparse Core Ops, SparseCore 0:
  171.5 106.1 all-gather.1

commit v2 on v1

--- a/solution.py
+++ b/solution.py
@@ -128,7 +128,7 @@
 
 
 def receive_kernel(source, centers, arrived, surface, surf_rows, tiles, checks, table, stage, feat):
-    leaves = tiles.shape[0] // 6
+    leaves = tiles.shape[0] // 8
     slots = leaves * TILE
     to_rows_table(arrived, table, slots // TILE, 6)
     table[pl.ds(slots, 8), :] = jnp.zeros((8, LANES), F32)
@@ -142,7 +142,10 @@
 
     def check(leaf, slot):
         rows = stage[slot * TILE : slot * TILE + TILE, 0:8].T
-        tiles[pl.ds(leaf * 6, 6), :] = rows[0:6]
+        at = [rows[c : c + 1] for c in range(6)]
+        size = at[0] * at[0] + at[1] * at[1] + at[2] * at[2] + 0.5 * SOFTENING
+        along = at[0] * at[3] + at[1] * at[4] + at[2] * at[5]
+        tiles[pl.ds(aligned(leaf, 8), 8), :] = jnp.concatenate([rows[0:6], size, -along])
         x_rows = [rows[c : c + 1] - centers[c * leaves + leaf] for c in range(3)]
         g_rows = [rows[3 + c : 4 + c] for c in range(3)]
 
@@ -180,68 +183,75 @@
     lax.fori_loop(0, leaves // 2, pair, 0)
 
 
-def near_kernel(listed, places, centers, own, extended, *rest):
-    before = rest[0] if len(rest) == 3 else None
-    out, target = rest[-2:]
-    leaves = own.shape[0] // 6
+def triple_split(value):
+    first = value.astype(BF16).astype(F32)
+    rest = value - first
+    second = rest.astype(BF16).astype(F32)
+    return first, second, (rest - second).astype(BF16).astype(F32)
+
+
+def row_at(value, row):
+    return jnp.broadcast_to(value[row : row + 1], (8, LANES))
+
+
+def near_kernel(listed, places, own, extended, *rest):
+    before = rest[0] if len(rest) == 2 else None
+    out = rest[-1]
+    leaves = own.shape[0] // 8
+    row = lax.broadcasted_iota(jnp.int32, (8, LANES), 0)
+    zero = jnp.zeros((8, LANES), F32)
+    one_row = jnp.ones((8, LANES), F32)
 
     def one(leaf, carry):
-        shift = [centers[c * leaves + leaf] for c in range(3)]
-        rows = own[pl.ds(leaf * 6, 6), :]
-        target[:, 0:6] = rows.T
-        y_rows = [own[pl.ds(leaf * 6 + c, 1), :] - shift[c] for c in range(3)]
-        left_d, left_w, sources = [], [], []
+        mine = own[pl.ds(aligned(leaf, 8), 8), :]
+        parts = triple_split(mine)
+        dist, push = [], []
+        for part in parts:
+            dist.append(jnp.where(row < 3, -2.0 * part, zero))
+            turned = pltpu.roll(part, 3, 0)
+            push.append(jnp.where((row >= 3) & (row < 6), turned, zero))
+        dist_one = jnp.where(row == 6, 1.0, dist[0])
+        push_one = jnp.where(row == 7, 1.0, push[0])
+        squares = jnp.where(row == 0, row_at(parts[0], 6), zero)
+        squares = jnp.where(row == 1, row_at(parts[1], 6), squares)
+        squares = jnp.where(row == 2, row_at(parts[2], 6), squares)
+        left = [dist_one] * 3 + [dist[1]] * 2 + [dist[2], squares, zero]
+        right = [push_one] * 3 + [push[1]] * 2 + [push[2], zero, zero]
+        targets = jnp.concatenate(
+            [jnp.concatenate(left).astype(BF16), jnp.concatenate(right).astype(BF16)], axis=1
+        )
+        sums = jnp.zeros((16, 2 * LANES), F32)
         for n in range(listed):
-            place = places[n * leaves + leaf] * 6
-            tile = [extended[pl.ds(place + c, 1), :] for c in range(6)]
-            sources.append([jnp.broadcast_to(row, (8, LANES)) for row in tile])
-            grow = [split_bf16(tile[3 + c]) for c in range(3)]
-            xrow = [split_bf16(tile[c] - shift[c]) for c in range(3)]
-            ones = jnp.ones((1, LANES), BF16)
-            zero = jnp.zeros((1, LANES), BF16)
-            left_d.append(jnp.concatenate([g[0] for g in grow] + [g[1] for g in grow] + [zero] * 10))
-            left_w.append(
-                jnp.concatenate([x[0] for x in xrow] + [x[1] for x in xrow] + [ones] + [zero] * 9)
+            tile = extended[pl.ds(aligned(places[n * leaves + leaf], 8), 8), :]
+            high, mid, low = triple_split(tile)
+            sources = jnp.concatenate([high, mid, low, high, mid, high, one_row, zero]).astype(BF16)
+            pairs = lax.dot_general(
+                sources, targets, (((0,), (0,)), ((), ())), preferred_element_type=F32
             )
-        sum_d = jnp.zeros((16, TILE), F32)
-        sum_w = jnp.zeros((16, TILE), F32)
-        sum_dl = jnp.zeros((16, TILE), F32)
-        sum_wl = jnp.zeros((16, TILE), F32)
-        directs = [[] for _ in range(listed)]
-        pushes = [[] for _ in range(listed)]
-        for block in range(TILE // 8):
-            y = [
-                jnp.broadcast_to(target[8 * block : 8 * block + 8, c : c + 1], (8, LANES))
-                for c in range(3)
-            ]
-            for n in range(listed):
-                x = sources[n]
-                dx, dy, dz = y[0] - x[0], y[1] - x[1], y[2] - x[2]
-                cube, direct = pair_weights(dx, dy, dz)
-                directs[n].append(direct)
-                pushes[n].append(cube * ((x[3] * dx + x[4] * dy) + x[5] * dz))
-        for n in range(listed):
-            dir_high, dir_low = split_bf16(jnp.concatenate(directs[n]))
-            push_high, push_low = split_bf16(jnp.concatenate(pushes[n]))
-            sum_d = sum_d + dot_nt(left_d[n], dir_high)
-            sum_dl = sum_dl + dot_nt(left_d[n], dir_low)
-            sum_w = sum_w + dot_nt(left_w[n], push_high)
-            sum_wl = sum_wl + dot_nt(left_w[n], push_low)
-        whole = sum_w[6:7] + sum_wl[6:7]
-        for c in range(3):
-            direct = sum_d[c : c + 1] + sum_d[3 + c : 4 + c] + sum_dl[c : c + 1]
-            moved = sum_w[c : c + 1] + sum_w[3 + c : 4 + c] + sum_wl[c : c + 1]
-            total = direct + (y_rows[c] * whole - moved)
-            if before is not None:
-                total = total + before[pl.ds(leaf * 3 + c, 1), :]
-            out[pl.ds(leaf * 3 + c, 1), :] = total
-        return carry
-
-    lax.fori_loop(0, leaves, one, 0)
+            root = lax.rsqrt(pairs[:, :LANES])
+            cube = root * root * root
+            direct = root + SOFTENING * cube
+            both = jnp.concatenate([direct, cube * pairs[:, LANES:]], axis=1)
+            both_high, both_low = split_bf16(both)
+            weights = jnp.concatenate([jnp.where(row == 6, 1.0, high), jnp.where(row == 6, 0.0, mid)])
+            weights = weights.astype(BF16)
+            sums = sums + dot_nn(
+                jnp.concatenate([weights, weights], axis=1),
+                jnp.concatenate([both_high, both_low], axis=0),
+            )
+        total = sums[0:8] + sums[8:16]
+        moved = total[:, LANES:]
+        flow = pltpu.roll(total[:, :LANES], 5, 0) + (mine * row_at(moved, 6) - moved)
+        if before is not None:
+            flow = flow + before[pl.ds(aligned(leaf, 8), 8), :]
+        out[pl.ds(aligned(leaf, 8), 8), :] = flow
+        return carry
+
+    lax.fori_loop(0, leaves, one, 0, unroll=2)
 
 
 def far_kernel(source, centers, own, near, local, surface, surf_rows, out, table, stage, feat):
-    leaves = own.shape[0] // 6
+    leaves = own.shape[0] // 8
     scale = 1.0 / (8.0 * math.pi)
     feat[...] = jnp.zeros(feat.shape, F32)
     stage[...] = jnp.zeros(stage.shape, F32)
@@ -253,7 +263,7 @@
         move_rows(write, source, leaf)
 
     def far(leaf, slot):
-        y_rows = [own[pl.ds(leaf * 6 + c, 1), :] - centers[c * leaves + leaf] for c in range(3)]
+        y_rows = [own[pl.ds(leaf * 8 + c, 1), :] - centers[c * leaves + leaf] for c in range(3)]
         g_rows = [local[pl.ds(leaf * 3 + c, 1), :] for c in range(3)]
         x_rows = [surf_rows[c : c + 1, :] for c in range(3)]
 
@@ -275,7 +285,7 @@
         sums = sums + dot_nn(low[0:16], cube_high) + dot_nn(high[16:32], dir_high)
         sums = sums + dot_nn(high[16:32], dir_low) + dot_nn(low[16:32], dir_high)
         flows = combine(sums, y_rows)
-        total = [(flows[c] + near[pl.ds(leaf * 3 + c, 1), :]) * scale for c in range(3)]
+        total = [(flows[c] + near[pl.ds(leaf * 8 + c, 1), :]) * scale for c in range(3)]
         for c in range(3):
             feat[64 + slot * 8 + c : 65 + slot * 8 + c, :] = total[c]
         stage[slot * TILE : slot * TILE + TILE, 0:8] = feat[64 + slot * 8 : 72 + slot * 8, :].T
@@ -314,19 +324,18 @@
     return blocks.reshape(rows.shape)
 
 
-def near_sum(listed, places, centers, tiles, extended, before):
+def near_sum(listed, places, tiles, extended, before):
     return pl.pallas_call(
         functools.partial(near_kernel, listed),
-        out_shape=jax.ShapeDtypeStruct((tiles.shape[0] // 2, LANES), F32),
-        in_specs=[SMEM, SMEM, VMEM, VMEM] + [VMEM] * len(before),
+        out_shape=jax.ShapeDtypeStruct(tiles.shape, F32),
+        in_specs=[SMEM, VMEM, VMEM] + [VMEM] * len(before),
         out_specs=VMEM,
-        scratch_shapes=[pltpu.VMEM((TILE, LANES), F32)],
         compiler_params=params(),
         cost_estimate=pl.CostEstimate(
             flops=listed * 10**10, transcendentals=0, bytes_accessed=10**7
         ),
         name=f"near{listed}",
-    )(places, centers, tiles, extended, *before)
+    )(places, tiles, extended, *before)
 
 
 def halo(shard, devices):
@@ -389,7 +398,7 @@
     surface = jnp.broadcast_to(surf_rows[:3, :SURF_PAD, None], (3, SURF_PAD, LANES))
     tiles, checks = pl.pallas_call(
         receive_kernel,
-        out_shape=[shape((6 * leaves, LANES), F32), shape((3 * leaves, LANES), F32)],
+        out_shape=[shape((8 * leaves, LANES), F32), shape((3 * leaves, LANES), F32)],
         in_specs=[SMEM, SMEM, VMEM, VMEM, VMEM],
         out_specs=[VMEM, VMEM],
         scratch_shapes=[
@@ -410,9 +419,9 @@
     moment = jnp.pad(moment, (0, 8 * LANES - expansion)).reshape(8, LANES)
     coarse = lax.all_gather(moment, ("gx", "gy"), axis=0, tiled=True)
 
-    near = near_sum(1, jnp.arange(leaves), centers, tiles, tiles, [])
+    near = near_sum(1, jnp.arange(leaves), tiles, tiles, [])
     places = (neighbours[0, 1:] - first).reshape(2 * leaves)
-    near = near_sum(2, places, centers, tiles, extended, [near])
+    near = near_sum(2, places, tiles, extended, [near])
 
     near, coarse, multipole_ext = lax.optimization_barrier((near, coarse, multipole_ext))
     coarse = coarse.reshape(-1, 8, LANES)[:, :2].reshape(-1, 2 * LANES)[:, :expansion]

time: 573 us -> 447 us (0.78)
  Pallas kernels: 422 us -> 294 us
    pallas_call x2, Pallas kernels: 243 us -> 114 us  [near_sum(): pl.pallas_call(functools.partial(near_kernel, listed), out_shape=jax.Shap...]
  transfers between devices with their start and end apart: 6 -> 6, of which waited for: 1 -> 1; matrix products, arithmetic and copies ran while one was open for 3% -> 4% of each run, Pallas kernels for 43% -> 26%
where the time goes in v2:
time: 447 us; the launch traced here: 444 us
  Pallas kernels  294 us (66%)
  local copies, waits for them, and re-layouts  35.2 us (8%)
  starting transfers between devices  28.6 us (6%)
  blocking collectives  24.8 us (6%)
  matrix products  21.1 us (5%)
  waiting for transfers between devices  15.5 us (3%)
  between operations  13.6 us (3%)
  other arithmetic  11.4 us (3%)
    pallas_call x2, Pallas kernels, near_sum(): pl.pallas_call(functools.partial(near_kernel, listed), out_shape=jax.Shap...  114 us
    pallas_call x1, Pallas kernels, body(): pl.pallas_call(receive_kernel, out_shape=[shape((8 * leaves, LANES), F32)...  74.8 us
    pallas_call x1, Pallas kernels, body(): pl.pallas_call(far_kernel, out_shape=shape((3 * slots // LANES, LANES), F...  62.5 us
    all_to_all x1, blocking collectives, exchange(): lax.all_to_all(blocks, 'gx', split_axis=0, concat_axis=0, tiled=True)  24.8 us
    pallas_call x1, Pallas kernels, body(): pl.pallas_call(return_kernel, out_shape=shape((8, count), F32), in_specs=...  21.9 us
    pallas_call x1, Pallas kernels, body(): pl.pallas_call(send_kernel, out_shape=shape((6 * slots // LANES, LANES),...  20.4 us
    all_to_all x1, starting transfers between devices, exchange(): lax.all_to_all(blocks, 'gx', split_axis=0, concat_axis=0, tiled=True)  16.3 us
    all_to_all x1, waiting for transfers between devices, exchange(): lax.all_to_all(blocks, 'gx', split_axis=0, concat_axis=0, tiled=True)  15.5 us
  transfers between devices with their start and end apart: 6, of which 1 were waited for; matrix products, arithmetic and copies ran while one was open for 4% of the time, Pallas kernels for 26%

profile of v2, /device:TPU:1, one launch (start us, length us, event | category | flops | bytes accessed | tf_op | source)
XLA Modules:
  0.0 443.8 jit_solution(12117181380264221322)
XLA Ops:
  6.5 1.1 copy.53
  7.6 1.2 reduce.3
  8.8 1.2 reduce.2
  10.1 2.3 fusion.10
  12.7 2.3 convolution_multiply_fusion
  15.3 0.7 reduce.dest
  16.1 0.8 maximum_maximum_fusion.packed
  16.9 20.4 %send.1 = f32[1536,128]{1,0:T(8,128)} custom-call(s32[8704]{0:T(1024)} %reduce.dest, f32[8,8704]{1,0:T(8,128)} %maximum_maximum_fusion.packed), custom_call_target="tpu_custom_call" | custom-call | tf_op jit(solution)/shard_map/send/pallas_call | solution.py:383
  37.2 16.3 %all-to-all-start = ((f32[128,1,1536]{2,1,0:T(1,128)}), f32[128,1,1536]{2,1,0:T(1,128)S(1)}, u32[]{:S(2)}, u32[]{:S(2)}) async-start(f32[128,1,1536]{2,1,0:T(1,128)} %bitcast.62), calls=%async_computation | async-start | bytes 1572864 | tf_op jit(solution)/shard_map/all_to_all | solution.py:323
  54.9 0.6 reshape.136.centers
  55.5 0.7 compare_and_fusion
  56.2 0.7 copy.32
  57.0 0.8 copy.33
  57.8 1.0 reshape.157
  58.8 1.5 copy.31
  60.3 1.3 pad_slice_fusion
  61.5 1.3 slice_subtract_fusion
  62.8 15.5 %all-to-all-done = f32[128,1,1536]{2,1,0:T(1,128)S(1)} async-done(((f32[128,1,1536]{2,1,0:T(1,128)}), f32[128,1,1536]{2,1,0:T(1,128)S(1)}, u32[]{:S(2)}, u32[]{:S(2)}) %all-to-all-start) | async-done | bytes 786464 | tf_op jit(solution)/shard_map/all_to_all | solution.py:323
  78.3 1.4 broadcast_in_dim.27.surface
  79.7 74.8 %receive.1 = (f32[2048,128]{1,0:T(8,128)}, f32[768,128]{1,0:T(8,128)}) custom-call(s32[32768]{0:T(1024)} %bitcast.70, f32[768]{0:T(1024)} %reshape.136.centers, f32[1536,128]{1,0:T(8,128)} %bitcast.61, f32[3,64,128]{2,1,0:T(8,128)} %broadcast_in_dim.27.surface, f32[8,128]{1,0:T(8,128)} %pad.12.surf_rows), custom_call_target="tpu_custom_call" | custom-call | tf_op jit(solution)/shard_map/receive/pallas_call | solution.py:399
  154.6 1.2 reshape.143
  155.7 0.9 copy.29
  156.6 1.5 fusion.11
  158.1 1.3 collective-permute-start.3
  159.4 4.7 %collective-permute-start.2 = (f32[256,168]{0,1:T(8,128)S(1)}, f32[256,168]{0,1:T(8,128)}, u32[]{:S(2)}, u32[]{:S(2)}) collective-permute-start(f32[256,168]{0,1:T(8,128)S(1)} %fusion.11), channel_id=1, source_target_pairs={{0,2},{2,4},{4,6},{6,8},{8,10},{10,12},{12,14},{14,16},{16,18},{18... | collective-permute-start | bytes 516104 | tf_op jit(solution)/shard_map/ppermute | solution.py:344
  164.2 1.3 collective-permute-start.1
  165.5 5.0 %collective-permute-start = (f32[2048,128]{1,0:T(8,128)}, f32[2048,128]{1,0:T(8,128)}, u32[]{:S(2)}, u32[]{:S(2)}) collective-permute-start(f32[2048,128]{1,0:T(8,128)} %get-tuple-element.10.own.extended), channel_id=1, source_target_pairs={{0,2},{2,4},{4,6},{6,8},{8,10},{10,12},{12,14},{14,16},{16,18},{18... | collective-permute-start | bytes 3145736 | tf_op jit(solution)/shard_map/ppermute | solution.py:344
  170.5 2.0 fusion.7
  172.5 0.6 pad_bitcast_fusion
  173.8 53.2 %near1.1.rest_0_ = f32[2048,128]{1,0:T(8,128)} custom-call(s32[256]{0:T(256)} %iota.21.places, f32[2048,128]{1,0:T(8,128)} %get-tuple-element.10.own.extended, f32[2048,128]{1,0:T(8,128)} %get-tuple-element.10.own.extended), custom_call_target="tpu_custom_call" | custom-call | flops 10000000000 | bytes 10000000 | tf_op jit(solution)/shard_map/near1/pallas_call | solution.py:328
  227.0 1.8 pad_maximum_fusion.1
  228.8 3.4 pad_maximum_fusion.extended
  232.3 60.9 %near2.1.near = f32[2048,128]{1,0:T(8,128)} custom-call(s32[512]{0:T(512)} %bitcast.77, f32[2048,128]{1,0:T(8,128)} %get-tuple-element.10.own.extended, f32[6144,128]{1,0:T(8,128)} %pad_maximum_fusion.extended, f32[2048,128]{1,0:T(8,128)} %near1.1.rest_0_), custom_call_target="tpu_custom_call" | custom-call | flops 20000000000 | bytes 10000000 | tf_op jit(solution)/shard_map/near2/pallas_call | solution.py:328
  293.1 1.4 slice.27
  294.9 1.3 convolution_bitcast_fusion.1
  296.2 1.2 fusion.12
  297.4 1.3 copy.34
  298.7 8.6 %gather_fusion = f32[2048,168]{1,0:T(8,128)} fusion(f32[768,168]{1,0:T(8,128)S(1)} %copy.34, s32[2048]{0:T(1024)S(1)} %broadcast_clamp_fusion), kind=kCustom, calls=%fused_computation | custom fusion | bytes 2760704 | tf_op jit(solution)/shard_map/jit(_take)/gather | solution.py:434
  307.3 5.9 %fusion = f32[256,16,168]{2,1,0:T(8,128)} fusion(f32[2048,168]{1,0:T(8,128)} %gather_fusion, pred[256,8]{1,0:T(8,128)(4,1)} %copy.32, s32[256,8]{1,0:T(8,128)} %copy.31), kind=kOutput, calls=%fused_computation.3 | convolution fusion | flops 66437120 | bytes 4139008 | tf_op jit(solution)/shard_map/nje,njk->nke/dot_general | solution.py:436
  313.2 5.5 %dot_general.34 = f32[32,8,2688]{2,1,0:T(8,128)} reshape(f32[256,16,168]{2,1,0:T(8,128)} %fusion) | data formatting | bytes 5505024 | tf_op jit(solution)/shard_map/dot_general | solution.py:437
  318.7 4.2 convolution_add_fusion
  323.2 0.9 pad.14
  324.1 2.0 reshape.151.local
  326.1 62.5 %far.1 = f32[768,128]{1,0:T(8,128)} custom-call(s32[32768]{0:T(1024)} %bitcast.71, f32[768]{0:T(1024)} %reshape.136.centers, f32[2048,128]{1,0:T(8,128)} %get-tuple-element.10.own.extended, f32[2048,128]{1,0:T(8,128)} %near2.1.near, f32[768,128]{1,0:T(8,128)} %reshape.151.local, f32[3,64,128]{2,1,0:T(8,128)} %broadcast_in_dim.27.surface, f32[8,128]{1,0:T(8,128)} %pad.12.surf_rows), custom_call_target="tpu_custom_call" | custom-call | tf_op jit(solution)/shard_map/far/pallas_call | solution.py:446
  388.6 24.8 %all_to_all.10 = f32[128,1,768]{2,1,0:T(1,128)} all-to-all(f32[128,1,768]{2,1,0:T(1,128)} %bitcast.64), channel_id=1, replica_groups=mesh['gx'=128,'gy'=2] {'gx'}, dimensions={0} | all-to-all | bytes 786432 | tf_op jit(solution)/shard_map/all_to_all | solution.py:323
  413.4 21.9 %back.1 = f32[8,8704]{1,0:T(8,128)} custom-call(s32[8704]{0:T(1024)} %reduce.dest, f32[768,128]{1,0:T(8,128)} %bitcast.65), custom_call_target="tpu_custom_call" | custom-call | tf_op jit(solution)/shard_map/back/pallas_call | solution.py:460
  435.2 1.0 slice_bitcast_fusion
  436.2 0.8 copy.37
  (45 shorter events, 3.5 us)
Async XLA Ops:
  6.5 288.3 %copy-start = (f32[16,168,168]{2,1,0:T(8,128)S(1)}, f32[16,168,168]{2,1,0:T(8,128)}, u32[]{:S(2)}) copy-start(f32[16,168,168]{2,1,0:T(8,128)} %param.26) | copy-start | bytes 5419012
  10.1 5.2 %copy-start.4 = (s32[1,8704]{1,0:T(1,128)S(1)}, s32[1,8704]{1,0:T(1,128)}, u32[]{:S(2)}) copy-start(s32[1,8704]{1,0:T(1,128)} %param.18) | copy-start | bytes 104452
  15.0 39.9 %copy-start.6 = (f32[3,1,256]{2,1,0:T(1,128)S(1)}, f32[3,1,256]{2,1,0:T(1,128)}, u32[]{:S(2)}) copy-start(f32[3,1,256]{2,1,0:T(1,128)} %param.19) | copy-start | bytes 9220
  37.2 41.1 %all-to-all-start = ((f32[128,1,1536]{2,1,0:T(1,128)}), f32[128,1,1536]{2,1,0:T(1,128)S(1)}, u32[]{:S(2)}, u32[]{:S(2)}) async-start(f32[128,1,1536]{2,1,0:T(1,128)} %bitcast.62), calls=%async_computation | async-start | bytes 1572864 | tf_op jit(solution)/shard_map/all_to_all | solution.py:323
  53.6 239.5 %all-gather.2.cloned.1.call-start = ((), (), s32[]{:S(2)}) async-start(), calls=%async_computation.2 | async-start | bytes 1052672 | tf_op jit(solution)/shard_map/all_gather | solution.py:420
  53.7 0.6 copy-start.5
  78.3 1.4 copy-start.3
  158.1 68.9 %collective-permute-start.3 = (f32[256,168]{0,1:T(8,128)S(1)}, f32[256,168]{0,1:T(8,128)}, u32[]{:S(2)}, u32[]{:S(2)}) collective-permute-start(f32[256,168]{0,1:T(8,128)S(1)} %fusion.11), channel_id=1, source_target_pairs={{2,0},{4,2},{6,4},{8,6},{10,8},{12,10},{14,12},{16,14},{18,16},{20... | collective-permute-start | bytes 516104 | tf_op jit(solution)/shard_map/ppermute | solution.py:345
  159.4 67.6 %collective-permute-start.2 = (f32[256,168]{0,1:T(8,128)S(1)}, f32[256,168]{0,1:T(8,128)}, u32[]{:S(2)}, u32[]{:S(2)}) collective-permute-start(f32[256,168]{0,1:T(8,128)S(1)} %fusion.11), channel_id=1, source_target_pairs={{0,2},{2,4},{4,6},{6,8},{8,10},{10,12},{12,14},{14,16},{16,18},{18... | collective-permute-start | bytes 516104 | tf_op jit(solution)/shard_map/ppermute | solution.py:344
  164.2 64.6 %collective-permute-start.1 = (f32[2048,128]{1,0:T(8,128)}, f32[2048,128]{1,0:T(8,128)}, u32[]{:S(2)}, u32[]{:S(2)}) collective-permute-start(f32[2048,128]{1,0:T(8,128)} %get-tuple-element.10.own.extended), channel_id=1, source_target_pairs={{2,0},{4,2},{6,4},{8,6},{10,8},{12,10},{14,12},{16,14},{18,16},{20... | collective-permute-start | bytes 3145736 | tf_op jit(solution)/shard_map/ppermute | solution.py:345
  165.5 63.3 %collective-permute-start = (f32[2048,128]{1,0:T(8,128)}, f32[2048,128]{1,0:T(8,128)}, u32[]{:S(2)}, u32[]{:S(2)}) collective-permute-start(f32[2048,128]{1,0:T(8,128)} %get-tuple-element.10.own.extended), channel_id=1, source_target_pairs={{0,2},{2,4},{4,6},{6,8},{8,10},{10,12},{12,14},{14,16},{16,18},{18... | collective-permute-start | bytes 3145736 | tf_op jit(solution)/shard_map/ppermute | solution.py:344
  173.7 55.1 %copy-start.2 = (f32[2048,128]{1,0:T(8,128)S(1)}, f32[2048,128]{1,0:T(8,128)}, u32[]{:S(2)}) copy-start(f32[2048,128]{1,0:T(8,128)} %get-tuple-element.10.own.extended) | copy-start | bytes 3145732
  232.3 62.3 %copy-start.7 = (s32[1,1,256]{2,1,0:T(1,128)S(1)}, s32[1,1,256]{2,1,0:T(1,128)}, u32[]{:S(2)}) copy-start(s32[1,1,256]{2,1,0:T(1,128)} %param.24) | copy-start | bytes 3076
  293.1 3.0 copy-start.1
Sparse Core Ops, SparseCore 0:
  173.3 105.8 all-gather.1

commit v3 on v2

--- a/solution.py
+++ b/solution.py
@@ -14,6 +14,7 @@
 LANES = 128
 SURF = 56
 SURF_PAD = 64
+GROUP = 4
 SOFTENING = 0.25
 RADIUS = 2.5
 HIGHEST = lax.Precision.HIGHEST
@@ -22,6 +23,7 @@
 
 VMEM = pl.BlockSpec(memory_space=pltpu.VMEM)
 SMEM = pl.BlockSpec(memory_space=pltpu.SMEM)
+ANY = pl.BlockSpec(memory_space=pl.ANY)
 
 
 def params():
@@ -55,9 +57,10 @@
 
 
 def move_rows(write, indices, block):
-    part = indices.at[pl.ds(block * TILE, TILE)]
-    for row in range(TILE):
-        write(row, part[row])
+    for start in range(0, TILE, 8):
+        part = indices.at[pl.ds(block * TILE + start, 8)]
+        for row in range(8):
+            write(start + row, part[row])
 
 
 def to_rows_table(source, table, blocks, width):
@@ -66,7 +69,7 @@
         table[pl.ds(aligned(block, TILE), TILE), 0:width] = rows.T
         return carry
 
-    lax.fori_loop(0, blocks, one, 0, unroll=4)
+    lax.fori_loop(0, blocks, one, 0, unroll=8)
 
 
 def from_rows_table(table, out, blocks, width):
@@ -75,7 +78,7 @@
         out[pl.ds(block * width, width), :] = rows[0:width]
         return carry
 
-    lax.fori_loop(0, blocks, one, 0, unroll=4)
+    lax.fori_loop(0, blocks, one, 0, unroll=8)
 
 
 def send_kernel(dest, packed, out, table, stage):
@@ -170,17 +173,25 @@
         for c in range(3):
             checks[pl.ds(leaf * 3 + c, 1), 0:SURF_PAD] = flows[c]
 
-    gather(0, 0)
-
-    def pair(step, carry):
-        leaf = step * 2
-        gather(leaf + 1, 1)
-        check(leaf, 0)
-        gather(jnp.minimum(leaf + 2, leaves - 1), 0)
-        check(leaf + 1, 1)
-        return carry
-
-    lax.fori_loop(0, leaves // 2, pair, 0)
+    def first_group(j, carry):
+        gather(j, j)
+        return carry
+
+    lax.fori_loop(0, GROUP, first_group, 0)
+
+    def two_groups(step, carry):
+        leaf = step * 2 * GROUP
+        for j in range(GROUP):
+            gather(leaf + GROUP + j, GROUP + j)
+        for j in range(GROUP):
+            check(leaf + j, j)
+        for j in range(GROUP):
+            gather(jnp.minimum(leaf + 2 * GROUP + j, leaves - 1), j)
+        for j in range(GROUP):
+            check(leaf + GROUP + j, GROUP + j)
+        return carry
+
+    lax.fori_loop(0, leaves // (2 * GROUP), two_groups, 0)
 
 
 def triple_split(value):
@@ -194,9 +205,26 @@
     return jnp.broadcast_to(value[row : row + 1], (8, LANES))
 
 
-def near_kernel(listed, places, own, extended, *rest):
-    before = rest[0] if len(rest) == 2 else None
-    out = rest[-1]
+def near_own_kernel(own, out):
+    near_loop(1, None, own, own, None, out)
+
+
+def near_others_kernel(places, previous, following, own, before, out, extended, sems):
+    rows = own.shape[0]
+    copies = [
+        pltpu.make_async_copy(
+            ref.at[pl.ds(0, rows), :], extended.at[pl.ds(n * rows, rows), :], sems.at[n]
+        )
+        for n, ref in enumerate((previous, own, following))
+    ]
+    for copy in copies:
+        copy.start()
+    for copy in copies:
+        copy.wait()
+    near_loop(2, places, own, extended, before, out)
+
+
+def near_loop(listed, places, own, extended, before, out):
     leaves = own.shape[0] // 8
     row = lax.broadcasted_iota(jnp.int32, (8, LANES), 0)
     zero = jnp.zeros((8, LANES), F32)
@@ -222,8 +250,11 @@
         )
         sums = jnp.zeros((16, 2 * LANES), F32)
         for n in range(listed):
-            tile = extended[pl.ds(aligned(places[n * leaves + leaf], 8), 8), :]
-            high, mid, low = triple_split(tile)
+            if places is None:
+                high, mid, low = parts
+            else:
+                place = places[n * leaves + leaf]
+                high, mid, low = triple_split(extended[pl.ds(aligned(place, 8), 8), :])
             sources = jnp.concatenate([high, mid, low, high, mid, high, one_row, zero]).astype(BF16)
             pairs = lax.dot_general(
                 sources, targets, (((0,), (0,)), ((), ())), preferred_element_type=F32
@@ -247,7 +278,7 @@
         out[pl.ds(aligned(leaf, 8), 8), :] = flow
         return carry
 
-    lax.fori_loop(0, leaves, one, 0, unroll=2)
+    lax.fori_loop(0, leaves, one, 0, unroll=8)
 
 
 def far_kernel(source, centers, own, near, local, surface, surf_rows, out, table, stage, feat):
@@ -287,20 +318,25 @@
         flows = combine(sums, y_rows)
         total = [(flows[c] + near[pl.ds(leaf * 8 + c, 1), :]) * scale for c in range(3)]
         for c in range(3):
-            feat[64 + slot * 8 + c : 65 + slot * 8 + c, :] = total[c]
-        stage[slot * TILE : slot * TILE + TILE, 0:8] = feat[64 + slot * 8 : 72 + slot * 8, :].T
-
-    far(0, 0)
-
-    def pair(step, carry):
-        leaf = step * 2
-        far(leaf + 1, 1)
-        scatter(leaf, 0)
-        far(jnp.minimum(leaf + 2, leaves - 1), 0)
-        scatter(leaf + 1, 1)
-        return carry
-
-    lax.fori_loop(0, leaves // 2, pair, 0)
+            feat[64 * GROUP + slot * 8 + c : 64 * GROUP + 1 + slot * 8 + c, :] = total[c]
+        stage[slot * TILE : slot * TILE + TILE, 0:8] = feat[64 * GROUP + slot * 8 : 64 * GROUP + 8 + slot * 8, :].T
+
+    for j in range(GROUP):
+        far(j, j)
+
+    def two_groups(step, carry):
+        leaf = step * 2 * GROUP
+        for j in range(GROUP):
+            far(leaf + GROUP + j, GROUP + j)
+        for j in range(GROUP):
+            scatter(leaf + j, j)
+        for j in range(GROUP):
+            far(jnp.minimum(leaf + 2 * GROUP + j, leaves - 1), j)
+        for j in range(GROUP):
+            scatter(leaf + GROUP + j, GROUP + j)
+        return carry
+
+    lax.fori_loop(0, leaves // (2 * GROUP), two_groups, 0)
     from_rows_table(table, out, out.shape[0] // 3, 3)
 
 
@@ -324,26 +360,38 @@
     return blocks.reshape(rows.shape)
 
 
-def near_sum(listed, places, tiles, extended, before):
+def near_own(tiles):
     return pl.pallas_call(
-        functools.partial(near_kernel, listed),
+        near_own_kernel,
         out_shape=jax.ShapeDtypeStruct(tiles.shape, F32),
-        in_specs=[SMEM, VMEM, VMEM] + [VMEM] * len(before),
+        in_specs=[VMEM],
         out_specs=VMEM,
         compiler_params=params(),
-        cost_estimate=pl.CostEstimate(
-            flops=listed * 10**10, transcendentals=0, bytes_accessed=10**7
-        ),
-        name=f"near{listed}",
-    )(places, tiles, extended, *before)
+        cost_estimate=pl.CostEstimate(flops=10**10, transcendentals=0, bytes_accessed=10**7),
+        name="near1",
+    )(tiles)
+
+
+def near_others(places, previous, following, tiles, before):
+    return pl.pallas_call(
+        near_others_kernel,
+        out_shape=jax.ShapeDtypeStruct(tiles.shape, F32),
+        in_specs=[SMEM, ANY, ANY, VMEM, VMEM],
+        out_specs=VMEM,
+        scratch_shapes=[
+            pltpu.VMEM((3 * tiles.shape[0], LANES), F32),
+            pltpu.SemaphoreType.DMA((3,)),
+        ],
+        compiler_params=params(),
+        cost_estimate=pl.CostEstimate(flops=2 * 10**10, transcendentals=0, bytes_accessed=10**7),
+        name="near2",
+    )(places, previous, following, tiles, before)
 
 
 def halo(shard, devices):
     up = [(i, i + 1) for i in range(devices - 1)]
     down = [(i + 1, i) for i in range(devices - 1)]
-    before = lax.ppermute(shard, "gx", up)
-    after = lax.ppermute(shard, "gx", down)
-    return jnp.concatenate([before, shard, after], axis=0)
+    return lax.ppermute(shard, "gx", up), lax.ppermute(shard, "gx", down)
 
 
 def body(
@@ -403,27 +451,35 @@
         out_specs=[VMEM, VMEM],
         scratch_shapes=[
             pltpu.VMEM((slots + 8, LANES), F32),
-            pltpu.VMEM((2 * TILE, LANES), F32),
-            pltpu.VMEM((64, LANES), F32),
+            pltpu.VMEM((2 * GROUP * TILE, LANES), F32),
+            pltpu.VMEM((2 * GROUP * 32, LANES), F32),
         ],
         compiler_params=params(),
         name="receive",
     )(source, centers, arrived, surface, surf_rows)
 
-    extended = halo(tiles, owners)
     check = checks.reshape(leaves, 3, LANES)[:, :, :SURF].reshape(leaves, expansion)
     multipole = jnp.dot(check, up_pinv, precision=HIGHEST, preferred_element_type=F32)
-    multipole_ext = halo(multipole, owners)
+    halves = [multipole[:, :LANES], jnp.pad(multipole[:, LANES:], ((0, 0), (0, 2 * LANES - expansion)))]
+    previous, following = halo(jnp.concatenate([tiles] + halves, axis=0), owners)
     grouped = jnp.sum(multipole.reshape(leaves // 8, 8, expansion), axis=0)
     moment = jnp.einsum("ce,cef->f", grouped, child_ops, precision=HIGHEST)
     moment = jnp.pad(moment, (0, 8 * LANES - expansion)).reshape(8, LANES)
     coarse = lax.all_gather(moment, ("gx", "gy"), axis=0, tiled=True)
 
-    near = near_sum(1, jnp.arange(leaves), tiles, tiles, [])
+    near = near_own(tiles)
     places = (neighbours[0, 1:] - first).reshape(2 * leaves)
-    near = near_sum(2, places, tiles, extended, [near])
-
-    near, coarse, multipole_ext = lax.optimization_barrier((near, coarse, multipole_ext))
+    near = near_others(places, previous, following, tiles, near)
+    near, coarse, previous, following = lax.optimization_barrier(
+        (near, coarse, previous[8 * leaves :], following[8 * leaves :])
+    )
+    multipole_ext = jnp.concatenate(
+        [
+            jnp.concatenate([previous[:leaves], halves[0], following[:leaves]], axis=0),
+            jnp.concatenate([previous[leaves:], halves[1], following[leaves:]], axis=0),
+        ],
+        axis=1,
+    )
     coarse = coarse.reshape(-1, 8, LANES)[:, :2].reshape(-1, 2 * LANES)[:, :expansion]
     op_ids = jnp.arange(NOPS)
     onehot = (coarse_op[0, 0][:, None] == op_ids[None, :]).astype(F32)
@@ -431,7 +487,7 @@
     coarse_local = jnp.einsum("ke,kef->f", by_op, trans_ops, precision=HIGHEST)
     pushed = jnp.einsum("cfe,e->cf", child_ops, coarse_local, precision=HIGHEST)
 
-    picked = jnp.take(multipole_ext, (inter_leaf[0] - first).T, axis=0)
+    picked = jnp.take(multipole_ext, (inter_leaf[0] - first).T, axis=0)[:, :, :expansion]
     leaf_hot = (inter_op[0].T[:, :, None] == op_ids[None, None, :]).astype(F32)
     leaf_by_op = jnp.einsum("nje,njk->nke", picked, leaf_hot, precision=HIGHEST)
     local = jnp.dot(
@@ -450,8 +506,8 @@
         out_specs=VMEM,
         scratch_shapes=[
             pltpu.VMEM((slots + 8, LANES), F32),
-            pltpu.VMEM((2 * TILE, LANES), F32),
-            pltpu.VMEM((80, LANES), F32),
+            pltpu.VMEM((2 * GROUP * TILE, LANES), F32),
+            pltpu.VMEM((2 * GROUP * 40, LANES), F32),
         ],
         compiler_params=params(),
         name="far",

time: 447 us -> 360 us (0.81)
  Pallas kernels: 294 us -> 168 us
  waiting for transfers between devices: 15.5 us -> 64.3 us
  starting transfers between devices: 28.6 us -> 22.7 us
  other arithmetic: 11.4 us -> 6.46 us
    pallas_call x2, Pallas kernels: 114 us -> 53.2 us  [the longest x1 31.9 us: near_others(): pl.pallas_call(near_others_kernel, out_shape=jax.ShapeDtypeStruct(tiles.s...]
    all_gather x1, waiting for transfers between devices: 0.01 us -> 45.1 us  [body(): coarse = lax.all_gather(moment, ('gx', 'gy'), axis=0, tiled=True)]
    pallas_call x1, Pallas kernels: 74.8 us -> 43.7 us  [body(): pl.pallas_call(receive_kernel, out_shape=[shape((8 * leaves, LANES), F32)...]
    pallas_call x1, Pallas kernels: 62.5 us -> 35.4 us  [body(): pl.pallas_call(far_kernel, out_shape=shape((3 * slots // LANES, LANES), F...]
    ppermute x4 -> x2, starting transfers between devices: 12.2 us -> 6.37 us  [halo(): return (lax.ppermute(shard, 'gx', up), lax.ppermute(shard, 'gx', down))]
  transfers between devices with their start and end apart: 6 -> 4, of which waited for: 1 -> 2; matrix products, arithmetic and copies ran while one was open for 4% -> 3% of each run, Pallas kernels for 26% -> 15%
where the time goes in v3:
time: 360 us; the launch traced here: 359 us
  Pallas kernels  168 us (47%)
  waiting for transfers between devices  64.3 us (18%)
  local copies, waits for them, and re-layouts  33.7 us (9%)
  blocking collectives  28.5 us (8%)
  starting transfers between devices  22.7 us (6%)
  matrix products  21.2 us (6%)
  between operations  13.8 us (4%)
  other arithmetic  6.46 us (2%)
    all_gather x1, waiting for transfers between devices, body(): coarse = lax.all_gather(moment, ('gx', 'gy'), axis=0, tiled=True)  45.1 us
    pallas_call x1, Pallas kernels, body(): pl.pallas_call(receive_kernel, out_shape=[shape((8 * leaves, LANES), F32)...  43.7 us
    pallas_call x1, Pallas kernels, body(): pl.pallas_call(far_kernel, out_shape=shape((3 * slots // LANES, LANES), F...  35.4 us
    pallas_call x1, Pallas kernels, near_others(): pl.pallas_call(near_others_kernel, out_shape=jax.ShapeDtypeStruct(tiles.s...  31.9 us
    all_to_all x1, blocking collectives, exchange(): lax.all_to_all(blocks, 'gx', split_axis=0, concat_axis=0, tiled=True)  28.5 us
    pallas_call x1, Pallas kernels, near_own(): pl.pallas_call(near_own_kernel, out_shape=jax.ShapeDtypeStruct(tiles.shap...  21.3 us
    all_to_all x1, waiting for transfers between devices, exchange(): lax.all_to_all(blocks, 'gx', split_axis=0, concat_axis=0, tiled=True)  19.2 us
    pallas_call x1, Pallas kernels, body(): pl.pallas_call(return_kernel, out_shape=shape((8, count), F32), in_specs=...  18 us
  transfers between devices with their start and end apart: 4, of which 2 were waited for; matrix products, arithmetic and copies ran while one was open for 3% of the time, Pallas kernels for 15%

profile of v3, /device:TPU:1, one launch (start us, length us, event | category | flops | bytes accessed | tf_op | source)
XLA Modules:
  0.0 358.5 jit_solution(6524844597151595931)
XLA Ops:
  6.5 1.1 copy.57
  7.6 1.2 reduce.3
  8.8 1.2 reduce.2
  10.1 2.3 fusion.12
  12.7 2.3 convolution_multiply_fusion
  15.4 0.7 reduce.dest
  16.1 0.8 maximum_maximum_fusion.1.packed
  16.9 17.6 %send.1 = f32[1536,128]{1,0:T(8,128)} custom-call(s32[8704]{0:T(1024)} %reduce.dest, f32[8,8704]{1,0:T(8,128)} %maximum_maximum_fusion.1.packed), custom_call_target="tpu_custom_call" | custom-call | tf_op jit(solution)/shard_map/send/pallas_call | solution.py:431
  34.5 16.3 %all-to-all-start = ((f32[128,1,1536]{2,1,0:T(1,128)}), f32[128,1,1536]{2,1,0:T(1,128)S(1)}, u32[]{:S(2)}, u32[]{:S(2)}) async-start(f32[128,1,1536]{2,1,0:T(1,128)} %bitcast.61), calls=%async_computation | async-start | bytes 1572864 | tf_op jit(solution)/shard_map/all_to_all | solution.py:359
  51.0 0.6 copy-done.9
  51.5 0.6 pad.16.surf_rows
  52.1 0.6 reshape.136.centers
  52.7 0.6 compare_and_fusion
  53.3 0.8 copy.37
  54.1 1.0 reshape.157
  55.1 1.3 pad_slice_fusion
  56.4 19.2 %all-to-all-done = f32[128,1,1536]{2,1,0:T(1,128)S(1)} async-done(((f32[128,1,1536]{2,1,0:T(1,128)}), f32[128,1,1536]{2,1,0:T(1,128)S(1)}, u32[]{:S(2)}, u32[]{:S(2)}) %all-to-all-start) | async-done | bytes 786464 | tf_op jit(solution)/shard_map/all_to_all | solution.py:359
  75.5 1.4 broadcast_in_dim.27.surface
  77.0 43.7 %receive.1 = (f32[2048,128]{1,0:T(8,128)}, f32[768,128]{1,0:T(8,128)}) custom-call(s32[32768]{0:T(1024)} %bitcast.69, f32[768]{0:T(1024)} %reshape.136.centers, f32[1536,128]{1,0:T(8,128)} %bitcast.60, f32[3,64,128]{2,1,0:T(8,128)} %broadcast_in_dim.27.surface, f32[8,128]{1,0:T(8,128)} %pad.16.surf_rows), custom_call_target="tpu_custom_call" | custom-call | tf_op jit(solution)/shard_map/receive/pallas_call | solution.py:447
  120.6 1.2 reshape.143
  122.0 1.7 bitcast_reduce_fusion
  123.8 1.1 pad_maximum_fusion
  124.9 1.3 collective-permute-start.1
  126.2 5.1 %collective-permute-start = (f32[2560,128]{1,0:T(8,128)}, f32[2560,128]{1,0:T(8,128)}, u32[]{:S(2)}, u32[]{:S(2)}) collective-permute-start(f32[2560,128]{1,0:T(8,128)} %pad_maximum_fusion), channel_id=1, source_target_pairs={{0,2},{2,4},{4,6},{6,8},{8,10},{10,12},{12,14},{14,16},{16,18},{18... | collective-permute-start | bytes 3932168 | tf_op jit(solution)/shard_map/ppermute | solution.py:394
  131.3 0.6 slice_subtract_fusion
  131.9 0.7 copy.36
  132.6 0.8 copy.35
  133.4 2.0 fusion.7
  135.4 0.6 pad_bitcast_fusion
  136.1 21.3 %near1.1.before = f32[2048,128]{1,0:T(8,128)} custom-call(f32[2048,128]{1,0:T(8,128)} %get-tuple-element.11.own), custom_call_target="tpu_custom_call" | custom-call | flops 10000000000 | bytes 10000000 | tf_op jit(solution)/shard_map/near1/pallas_call | solution.py:364
  157.4 1.0 slice.66
  158.4 1.0 slice.65
  159.4 31.9 %near2.1.near = f32[2048,128]{1,0:T(8,128)} custom-call(s32[512]{0:T(512)} %bitcast.76, f32[2560,128]{1,0:T(8,128)} %collective-permute-done.previous, f32[2560,128]{1,0:T(8,128)} %collective-permute-done.1.following, f32[2048,128]{1,0:T(8,128)} %get-tuple-element.11.own, f32[2048,128]{1,0:T(8,128)} %near1.1.before), custom_call_target="tpu_custom_call" | custom-call | flops 20000000000 | bytes 10000000 | tf_op jit(solution)/shard_map/near2/pallas_call | solution.py:376
  191.2 45.1 %all-gather.2.cloned.1.call-done = f32[2048,128]{1,0:T(8,128)} async-done(((f32[8,128]{1,0:T(8,128)}), f32[2048,128]{1,0:T(8,128)}) %all-gather.2.cloned.1.call-update) | async-done | bytes 1048592 | tf_op jit(solution)/shard_map/all_gather | solution.py:468
  236.4 1.4 slice.68
  238.1 1.3 convolution_bitcast_fusion.1
  239.4 1.2 fusion.13
  240.8 8.6 %gather_fusion = f32[2048,256]{1,0:T(8,128)} fusion(f32[768,256]{1,0:T(8,128)S(1)} %maximum_maximum_fusion, s32[2048]{0:T(1024)S(1)} %broadcast_clamp_fusion), kind=kCustom, calls=%fused_computation | custom fusion | bytes 4202496 | tf_op jit(solution)/shard_map/jit(_take)/gather | solution.py:490
  249.4 5.9 %fusion = f32[256,16,168]{2,1,0:T(8,128)} fusion(f32[256,8,256]{2,1,0:T(8,128)} %bitcast.59, pred[256,8]{1,0:T(8,128)(4,1)} %copy.36, s32[256,8]{1,0:T(8,128)} %copy.35), kind=kOutput, calls=%fused_computation.2 | convolution fusion | flops 66437120 | bytes 4859904 | tf_op jit(solution)/shard_map/nje,njk->nke/dot_general | solution.py:492
  255.3 5.4 %dot_general.34 = f32[32,8,2688]{2,1,0:T(8,128)} reshape(f32[256,16,168]{2,1,0:T(8,128)} %fusion) | data formatting | bytes 5505024 | tf_op jit(solution)/shard_map/dot_general | solution.py:493
  260.7 4.3 %convolution_add_fusion = f32[32,8,168]{2,1,0:T(8,128)S(1)} fusion(f32[32,8,2688]{2,1,0:T(8,128)} %dot_general.34, f32[2688,168,1]{1,0,2:T(8,128)S(1)} %bitcast.58, f32[8,168]{1,0:T(8,128)S(1)} %bitcast.73), kind=kOutput, calls=%fused_computation.4 | convolution fusion | flops 1387309056 | bytes 4736256 | tf_op jit(solution)/shard_map/dot_general | solution.py:493
  265.2 0.9 pad.19
  266.1 2.0 reshape.151.local
  268.1 35.4 %far.1 = f32[768,128]{1,0:T(8,128)} custom-call(s32[32768]{0:T(1024)} %bitcast.70, f32[768]{0:T(1024)} %reshape.136.centers, f32[2048,128]{1,0:T(8,128)} %get-tuple-element.11.own, f32[2048,128]{1,0:T(8,128)} %near2.1.near, f32[768,128]{1,0:T(8,128)} %reshape.151.local, f32[3,64,128]{2,1,0:T(8,128)} %broadcast_in_dim.27.surface, f32[8,128]{1,0:T(8,128)} %pad.16.surf_rows), custom_call_target="tpu_custom_call" | custom-call | tf_op jit(solution)/shard_map/far/pallas_call | solution.py:502
  303.5 28.5 %all_to_all.10 = f32[128,1,768]{2,1,0:T(1,128)} all-to-all(f32[128,1,768]{2,1,0:T(1,128)} %bitcast.63), channel_id=1, replica_groups=mesh['gx'=128,'gy'=2] {'gx'}, dimensions={0} | all-to-all | bytes 786432 | tf_op jit(solution)/shard_map/all_to_all | solution.py:359
  332.0 18.0 %back.1 = f32[8,8704]{1,0:T(8,128)} custom-call(s32[8704]{0:T(1024)} %reduce.dest, f32[768,128]{1,0:T(8,128)} %bitcast.64), custom_call_target="tpu_custom_call" | custom-call | tf_op jit(solution)/shard_map/back/pallas_call | solution.py:516
  349.9 1.0 slice_bitcast_fusion
  350.9 0.8 copy.40
  (60 shorter events, 1.9 us)
Async XLA Ops:
  6.5 231.6 %copy-start = (f32[16,168,168]{2,1,0:T(8,128)S(1)}, f32[16,168,168]{2,1,0:T(8,128)}, u32[]{:S(2)}) copy-start(f32[16,168,168]{2,1,0:T(8,128)} %param.26) | copy-start | bytes 5419012
  10.1 5.2 %copy-start.8 = (s32[1,8704]{1,0:T(1,128)S(1)}, s32[1,8704]{1,0:T(1,128)}, u32[]{:S(2)}) copy-start(s32[1,8704]{1,0:T(1,128)} %param.18) | copy-start | bytes 104452
  15.0 37.1 %copy-start.13 = (f32[3,1,256]{2,1,0:T(1,128)S(1)}, f32[3,1,256]{2,1,0:T(1,128)}, u32[]{:S(2)}) copy-start(f32[3,1,256]{2,1,0:T(1,128)} %param.19) | copy-start | bytes 9220
  15.0 37.8 %copy-start.12 = (s32[1,8,256]{2,1,0:T(8,128)S(1)}, s32[1,8,256]{2,1,0:T(8,128)}, u32[]{:S(2)}) copy-start(s32[1,8,256]{2,1,0:T(8,128)} %param.22) | copy-start | bytes 24580
  34.5 41.1 %all-to-all-start = ((f32[128,1,1536]{2,1,0:T(1,128)}), f32[128,1,1536]{2,1,0:T(1,128)S(1)}, u32[]{:S(2)}, u32[]{:S(2)}) async-start(f32[128,1,1536]{2,1,0:T(1,128)} %bitcast.61), calls=%async_computation | async-start | bytes 1572864 | tf_op jit(solution)/shard_map/all_to_all | solution.py:359
  50.8 185.6 %all-gather.2.cloned.1.call-start = ((), (), s32[]{:S(2)}) async-start(), calls=%async_computation.2 | async-start | bytes 1052672 | tf_op jit(solution)/shard_map/all_gather | solution.py:468
  50.9 0.6 copy-start.9
  75.5 1.4 copy-start.3
  122.0 1.8 copy-start.2
  122.0 9.3 %copy-start.14 = (s32[1,3,256]{2,0,1:T(1,128)S(1)}, s32[1,3,256]{2,0,1:T(1,128)}, u32[]{:S(2)}) copy-start(s32[1,3,256]{2,0,1:T(1,128)} %param.21) | copy-start | bytes 9220
  122.0 9.9 %copy-start.11 = (pred[256,8]{0,1:T(8,128)(4,1)S(1)}, pred[256,8]{0,1:T(8,128)(4,1)}, u32[]{:S(2)}) copy-start(pred[256,8]{0,1:T(8,128)(4,1)} %get-tuple-element.17) | copy-start | bytes 6148
  122.0 10.6 %copy-start.10 = (s32[1,8,256]{2,1,0:T(8,128)S(1)}, s32[1,8,256]{2,1,0:T(8,128)}, u32[]{:S(2)}) copy-start(s32[1,8,256]{2,1,0:T(8,128)} %param.23) | copy-start | bytes 24580
  123.7 1.2 copy-start.4
  123.7 2.5 copy-start.6
  124.9 32.5 %collective-permute-start.1 = (f32[2560,128]{1,0:T(8,128)}, f32[2560,128]{1,0:T(8,128)}, u32[]{:S(2)}, u32[]{:S(2)}) collective-permute-start(f32[2560,128]{1,0:T(8,128)} %pad_maximum_fusion), channel_id=1, source_target_pairs={{2,0},{4,2},{6,4},{8,6},{10,8},{12,10},{14,12},{16,14},{18,16},{20... | collective-permute-start | bytes 3932168 | tf_op jit(solution)/shard_map/ppermute | solution.py:394
  126.2 32.2 %collective-permute-start = (f32[2560,128]{1,0:T(8,128)}, f32[2560,128]{1,0:T(8,128)}, u32[]{:S(2)}, u32[]{:S(2)}) collective-permute-start(f32[2560,128]{1,0:T(8,128)} %pad_maximum_fusion), channel_id=1, source_target_pairs={{0,2},{2,4},{4,6},{6,8},{8,10},{10,12},{12,14},{14,16},{16,18},{18... | collective-permute-start | bytes 3932168 | tf_op jit(solution)/shard_map/ppermute | solution.py:394
  159.4 78.4 %copy-start.15 = (s32[1,1,256]{2,1,0:T(1,128)S(1)}, s32[1,1,256]{2,1,0:T(1,128)}, u32[]{:S(2)}) copy-start(s32[1,1,256]{2,1,0:T(1,128)} %param.24) | copy-start | bytes 3076
  236.4 3.1 copy-start.1
  238.1 2.6 copy-start.5
  238.1 2.6 copy-start.7
Sparse Core Ops, SparseCore 0:
  136.2 100.1 all-gather.1

commit v4 on v3

--- a/solution.py
+++ b/solution.py
@@ -14,7 +14,7 @@
 LANES = 128
 SURF = 56
 SURF_PAD = 64
-GROUP = 4
+GROUP = 8
 SOFTENING = 0.25
 RADIUS = 2.5
 HIGHEST = lax.Precision.HIGHEST
@@ -63,6 +63,32 @@
             write(start + row, part[row])
 
 
+def pipelined(total, group, first, second, rolled):
+    def start(j, carry):
+        first(j, j)
+        return carry
+
+    if rolled:
+        lax.fori_loop(0, group, start, 0)
+    else:
+        for j in range(group):
+            first(j, j)
+
+    def two_groups(step, carry):
+        base = step * 2 * group
+        for j in range(group):
+            first(base + group + j, group + j)
+        for j in range(group):
+            second(base + j, j)
+        for j in range(group):
+            first(jnp.minimum(base + 2 * group + j, total - 1), j)
+        for j in range(group):
+            second(base + group + j, group + j)
+        return carry
+
+    lax.fori_loop(0, total // (2 * group), two_groups, 0)
+
+
 def to_rows_table(source, table, blocks, width):
     def one(block, carry):
         rows = source[pl.ds(block * width, width), :]
@@ -84,16 +110,17 @@
 def send_kernel(dest, packed, out, table, stage):
     blocks = packed.shape[1] // LANES
 
-    def one(block, carry):
-        stage[:, 0:8] = packed[:, pl.ds(aligned(block, LANES), LANES)].T
-
+    def turn(block, slot):
+        columns = packed[:, pl.ds(aligned(block, LANES), LANES)]
+        stage[slot * TILE : slot * TILE + TILE, 0:8] = columns.T
+
+    def scatter(block, slot):
         def write(row, index):
-            table[pl.ds(index, 1), :] = stage[pl.ds(row, 1), :]
+            table[pl.ds(index, 1), :] = stage[pl.ds(slot * TILE + row, 1), :]
 
         move_rows(write, dest, block)
-        return carry
-
-    lax.fori_loop(0, blocks, one, 0)
+
+    pipelined(blocks, 2, turn, scatter, False)
     from_rows_table(table, out, out.shape[0] // 6, 6)
 
 
@@ -173,25 +200,7 @@
         for c in range(3):
             checks[pl.ds(leaf * 3 + c, 1), 0:SURF_PAD] = flows[c]
 
-    def first_group(j, carry):
-        gather(j, j)
-        return carry
-
-    lax.fori_loop(0, GROUP, first_group, 0)
-
-    def two_groups(step, carry):
-        leaf = step * 2 * GROUP
-        for j in range(GROUP):
-            gather(leaf + GROUP + j, GROUP + j)
-        for j in range(GROUP):
-            check(leaf + j, j)
-        for j in range(GROUP):
-            gather(jnp.minimum(leaf + 2 * GROUP + j, leaves - 1), j)
-        for j in range(GROUP):
-            check(leaf + GROUP + j, GROUP + j)
-        return carry
-
-    lax.fori_loop(0, leaves // (2 * GROUP), two_groups, 0)
+    pipelined(leaves, GROUP, gather, check, True)
 
 
 def triple_split(value):
@@ -281,7 +290,9 @@
     lax.fori_loop(0, leaves, one, 0, unroll=8)
 
 
-def far_kernel(source, centers, own, near, local, surface, surf_rows, out, table, stage, feat):
+def far_kernel(
+    source, centers, own, near, local, pushed, surface, surf_rows, out, table, stage, feat
+):
     leaves = own.shape[0] // 8
     scale = 1.0 / (8.0 * math.pi)
     feat[...] = jnp.zeros(feat.shape, F32)
@@ -295,7 +306,11 @@
 
     def far(leaf, slot):
         y_rows = [own[pl.ds(leaf * 8 + c, 1), :] - centers[c * leaves + leaf] for c in range(3)]
-        g_rows = [local[pl.ds(leaf * 3 + c, 1), :] for c in range(3)]
+        child = slot % 8
+        g_rows = [
+            local[pl.ds(leaf * 3 + c, 1), :] + pushed[child * 3 + c : child * 3 + c + 1, :]
+            for c in range(3)
+        ]
         x_rows = [surf_rows[c : c + 1, :] for c in range(3)]
 
         def store_a(row, value):
@@ -321,37 +336,26 @@
             feat[64 * GROUP + slot * 8 + c : 64 * GROUP + 1 + slot * 8 + c, :] = total[c]
         stage[slot * TILE : slot * TILE + TILE, 0:8] = feat[64 * GROUP + slot * 8 : 64 * GROUP + 8 + slot * 8, :].T
 
-    for j in range(GROUP):
-        far(j, j)
-
-    def two_groups(step, carry):
-        leaf = step * 2 * GROUP
-        for j in range(GROUP):
-            far(leaf + GROUP + j, GROUP + j)
-        for j in range(GROUP):
-            scatter(leaf + j, j)
-        for j in range(GROUP):
-            far(jnp.minimum(leaf + 2 * GROUP + j, leaves - 1), j)
-        for j in range(GROUP):
-            scatter(leaf + GROUP + j, GROUP + j)
-        return carry
-
-    lax.fori_loop(0, leaves // (2 * GROUP), two_groups, 0)
+    pipelined(leaves, GROUP, far, scatter, False)
     from_rows_table(table, out, out.shape[0] // 3, 3)
 
 
 def return_kernel(dest, arrived, out, table, stage):
     to_rows_table(arrived, table, arrived.shape[0] // 3, 3)
-
-    def one(block, carry):
+    blocks = out.shape[0] // 3
+
+    def gather(block, slot):
         def write(row, index):
-            stage[pl.ds(row, 1), :] = table[pl.ds(index, 1), :]
+            stage[pl.ds(slot * TILE + row, 1), :] = table[pl.ds(index, 1), :]
 
         move_rows(write, dest, block)
-        out[:, pl.ds(aligned(block, LANES), LANES)] = stage[:, 0:8].T
-        return carry
-
-    lax.fori_loop(0, out.shape[1] // LANES, one, 0)
+
+    def turn(block, slot):
+        rows = stage[slot * TILE : slot * TILE + TILE, 0:8].T
+        for c in range(3):
+            out[pl.ds(c * blocks + block, 1), :] = rows[c : c + 1]
+
+    pipelined(blocks, 2, gather, turn, True)
 
 
 def exchange(rows, owners):
@@ -433,7 +437,7 @@
         out_shape=shape((6 * slots // LANES, LANES), F32),
         in_specs=[SMEM, VMEM],
         out_specs=VMEM,
-        scratch_shapes=[pltpu.VMEM((slots, LANES), F32), pltpu.VMEM((TILE, LANES), F32)],
+        scratch_shapes=[pltpu.VMEM((slots, LANES), F32), pltpu.VMEM((4 * TILE, LANES), F32)],
         compiler_params=params(),
         name="send",
     )(point_dest.reshape(count), packed)
@@ -461,32 +465,25 @@
     check = checks.reshape(leaves, 3, LANES)[:, :, :SURF].reshape(leaves, expansion)
     multipole = jnp.dot(check, up_pinv, precision=HIGHEST, preferred_element_type=F32)
     halves = [multipole[:, :LANES], jnp.pad(multipole[:, LANES:], ((0, 0), (0, 2 * LANES - expansion)))]
-    previous, following = halo(jnp.concatenate([tiles] + halves, axis=0), owners)
     grouped = jnp.sum(multipole.reshape(leaves // 8, 8, expansion), axis=0)
     moment = jnp.einsum("ce,cef->f", grouped, child_ops, precision=HIGHEST)
     moment = jnp.pad(moment, (0, 8 * LANES - expansion)).reshape(8, LANES)
+    moment, *halves = lax.optimization_barrier((moment, *halves))
     coarse = lax.all_gather(moment, ("gx", "gy"), axis=0, tiled=True)
+    previous, following = halo(jnp.concatenate([tiles] + halves, axis=0), owners)
 
     near = near_own(tiles)
     places = (neighbours[0, 1:] - first).reshape(2 * leaves)
     near = near_others(places, previous, following, tiles, near)
-    near, coarse, previous, following = lax.optimization_barrier(
-        (near, coarse, previous[8 * leaves :], following[8 * leaves :])
-    )
+    sides = [previous[8 * leaves :], following[8 * leaves :]]
     multipole_ext = jnp.concatenate(
         [
-            jnp.concatenate([previous[:leaves], halves[0], following[:leaves]], axis=0),
-            jnp.concatenate([previous[leaves:], halves[1], following[leaves:]], axis=0),
+            jnp.concatenate([sides[0][:leaves], halves[0], sides[1][:leaves]], axis=0),
+            jnp.concatenate([sides[0][leaves:], halves[1], sides[1][leaves:]], axis=0),
         ],
         axis=1,
     )
-    coarse = coarse.reshape(-1, 8, LANES)[:, :2].reshape(-1, 2 * LANES)[:, :expansion]
     op_ids = jnp.arange(NOPS)
-    onehot = (coarse_op[0, 0][:, None] == op_ids[None, :]).astype(F32)
-    by_op = jnp.einsum("bk,be->ke", onehot, coarse, precision=HIGHEST)
-    coarse_local = jnp.einsum("ke,kef->f", by_op, trans_ops, precision=HIGHEST)
-    pushed = jnp.einsum("cfe,e->cf", child_ops, coarse_local, precision=HIGHEST)
-
     picked = jnp.take(multipole_ext, (inter_leaf[0] - first).T, axis=0)[:, :, :expansion]
     leaf_hot = (inter_op[0].T[:, :, None] == op_ids[None, None, :]).astype(F32)
     leaf_by_op = jnp.einsum("nje,njk->nke", picked, leaf_hot, precision=HIGHEST)
@@ -495,14 +492,22 @@
         trans_ops.reshape(NOPS * expansion, expansion),
         precision=HIGHEST,
         preferred_element_type=F32,
-    )
-    local = (local.reshape(leaves // 8, 8, expansion) + pushed[None]).reshape(leaves, 3, SURF)
+    ).reshape(leaves, 3, SURF)
     local = jnp.pad(local, ((0, 0), (0, 0), (0, LANES - SURF))).reshape(3 * leaves, LANES)
+
+    near, local, coarse = lax.optimization_barrier((near, local, coarse))
+    coarse = coarse.reshape(-1, 8, LANES)[:, :2].reshape(-1, 2 * LANES)[:, :expansion]
+    onehot = (coarse_op[0, 0][:, None] == op_ids[None, :]).astype(F32)
+    by_op = jnp.einsum("bk,be->ke", onehot, coarse, precision=HIGHEST)
+    coarse_local = jnp.einsum("ke,kef->f", by_op, trans_ops, precision=HIGHEST)
+    pushed = jnp.einsum("cfe,e->cf", child_ops, coarse_local, precision=HIGHEST)
+    pushed = jnp.pad(pushed.reshape(8, 3, SURF), ((0, 0), (0, 0), (0, LANES - SURF)))
+    pushed = pushed.reshape(24, LANES)
 
     returning = pl.pallas_call(
         far_kernel,
         out_shape=shape((3 * slots // LANES, LANES), F32),
-        in_specs=[SMEM, SMEM, VMEM, VMEM, VMEM, VMEM, VMEM],
+        in_specs=[SMEM, SMEM, VMEM, VMEM, VMEM, VMEM, VMEM, VMEM],
         out_specs=VMEM,
         scratch_shapes=[
             pltpu.VMEM((slots + 8, LANES), F32),
@@ -511,18 +516,18 @@
         ],
         compiler_params=params(),
         name="far",
-    )(source, centers, tiles, near, local, surface, surf_rows)
+    )(source, centers, tiles, near, local, pushed, surface, surf_rows)
     came_back = exchange(returning, owners)
     velocity = pl.pallas_call(
         return_kernel,
-        out_shape=shape((8, count), F32),
+        out_shape=shape((3 * count // LANES, LANES), F32),
         in_specs=[SMEM, VMEM],
         out_specs=VMEM,
-        scratch_shapes=[pltpu.VMEM((slots, LANES), F32), pltpu.VMEM((TILE, LANES), F32)],
+        scratch_shapes=[pltpu.VMEM((slots, LANES), F32), pltpu.VMEM((4 * TILE, LANES), F32)],
         compiler_params=params(),
         name="back",
     )(point_dest.reshape(count), came_back)
-    return velocity[:3].reshape(3, 1, count)
+    return velocity.reshape(3, 1, count)
 
 
 def solution(mesh):

time: 360 us -> 316 us (0.88)
  waiting for transfers between devices: 64.3 us -> 40.2 us
  Pallas kernels: 168 us -> 155 us
  matrix products: 21.2 us -> 17.5 us
    all_gather x1, waiting for transfers between devices: 45.1 us -> 18.9 us  [body(): coarse = lax.all_gather(moment, ('gx', 'gy'), axis=0, tiled=True)]
    dot_general x0 -> x1, local copies, waits for them, and re-layouts: none -> 5.13 us  [body(): leaf_by_op = jnp.einsum('nje,njk->nke', picked, leaf_hot, precision=HIGHEST)]
    pallas_call x1, Pallas kernels: 43.7 us -> 39.4 us  [body(): pl.pallas_call(receive_kernel, out_shape=[shape((8 * leaves, LANES), F32)...]
    pallas_call x1, Pallas kernels: 17.6 us -> 13.9 us  [body(): pl.pallas_call(send_kernel, out_shape=shape((6 * slots // LANES, LANES),...]
  transfers between devices with their start and end apart: 4 -> 4, of which waited for: 2 -> 3; matrix products, arithmetic and copies ran while one was open for 3% -> 10% of each run, Pallas kernels for 15% -> 17%
where the time goes in v4:
time: 316 us
  Pallas kernels  155 us (49%)
  waiting for transfers between devices  40.2 us (13%)
  local copies, waits for them, and re-layouts  33.3 us (11%)
  blocking collectives  28.5 us (9%)
  starting transfers between devices  22.7 us (7%)
  matrix products  17.5 us (6%)
  between operations  13.7 us (4%)
  other arithmetic  4.84 us (2%)
    pallas_call x1, Pallas kernels, body(): pl.pallas_call(receive_kernel, out_shape=[shape((8 * leaves, LANES), F32)...  39.4 us
    pallas_call x1, Pallas kernels, body(): pl.pallas_call(far_kernel, out_shape=shape((3 * slots // LANES, LANES), F...  33.2 us
    pallas_call x1, Pallas kernels, near_others(): pl.pallas_call(near_others_kernel, out_shape=jax.ShapeDtypeStruct(tiles.s...  31.8 us
    all_to_all x1, blocking collectives, exchange(): lax.all_to_all(blocks, 'gx', split_axis=0, concat_axis=0, tiled=True)  28.5 us
    pallas_call x1, Pallas kernels, near_own(): pl.pallas_call(near_own_kernel, out_shape=jax.ShapeDtypeStruct(tiles.shap...  21.3 us
    all_to_all x1, waiting for transfers between devices, exchange(): lax.all_to_all(blocks, 'gx', split_axis=0, concat_axis=0, tiled=True)  19.6 us
    all_gather x1, waiting for transfers between devices, body(): coarse = lax.all_gather(moment, ('gx', 'gy'), axis=0, tiled=True)  18.9 us
    all_to_all x1, starting transfers between devices, exchange(): lax.all_to_all(blocks, 'gx', split_axis=0, concat_axis=0, tiled=True)  16.3 us
  transfers between devices with their start and end apart: 4, of which 3 were waited for; matrix products, arithmetic and copies ran while one was open for 10% of the time, Pallas kernels for 17%

profile of v4, /device:TPU:1, one launch (start us, length us, event | category | flops | bytes accessed | tf_op | source)
XLA Modules:
  0.0 315.6 jit_solution(15661861753022351234)
XLA Ops:
  6.5 1.0 copy.65
  7.6 1.2 reduce.3
  8.8 1.3 reduce.2
  10.2 0.9 fusion.12
  11.5 0.9 convolution_multiply_fusion
  12.7 0.7 reduce.dest
  13.5 0.8 maximum_maximum_fusion.1.packed
  14.3 13.9 %send.1 = f32[1536,128]{1,0:T(8,128)} custom-call(s32[8704]{0:T(1024)} %reduce.dest, f32[8,8704]{1,0:T(8,128)} %maximum_maximum_fusion.1.packed), custom_call_target="tpu_custom_call" | custom-call | tf_op jit(solution)/shard_map/send/pallas_call | solution.py:435
  28.1 16.3 %all-to-all-start = ((f32[128,1,1536]{2,1,0:T(1,128)}), f32[128,1,1536]{2,1,0:T(1,128)S(1)}, u32[]{:S(2)}, u32[]{:S(2)}) async-start(f32[128,1,1536]{2,1,0:T(1,128)} %bitcast.65), calls=%async_computation | async-start | bytes 1572864 | tf_op jit(solution)/shard_map/all_to_all | solution.py:363
  44.6 0.6 reshape.139.centers
  45.2 0.6 pad.20.surf_rows
  46.1 0.2 copy.40
  46.4 3.2 %copy.43 = f32[168,2688]{1,0:T(8,128)} copy(f32[168,2688]{0,1:T(8,128)} %bitcast.61) | data formatting | bytes 3612672 | tf_op jit(solution)/shard_map/dot_general | solution.py:490
  49.6 19.6 %all-to-all-done = f32[128,1,1536]{2,1,0:T(1,128)S(1)} async-done(((f32[128,1,1536]{2,1,0:T(1,128)}), f32[128,1,1536]{2,1,0:T(1,128)S(1)}, u32[]{:S(2)}, u32[]{:S(2)}) %all-to-all-start) | async-done | bytes 786464 | tf_op jit(solution)/shard_map/all_to_all | solution.py:363
  69.2 0.9 broadcast_in_dim.26.surface
  70.2 39.4 %receive.1 = (f32[2048,128]{1,0:T(8,128)}, f32[768,128]{1,0:T(8,128)}) custom-call(s32[32768]{0:T(1024)} %bitcast.73, f32[768]{0:T(1024)} %reshape.139.centers, f32[1536,128]{1,0:T(8,128)} %bitcast.64, f32[3,64,128]{2,1,0:T(8,128)} %broadcast_in_dim.26.surface, f32[8,128]{1,0:T(8,128)} %pad.20.surf_rows), custom_call_target="tpu_custom_call" | custom-call | tf_op jit(solution)/shard_map/receive/pallas_call | solution.py:451
  109.6 1.2 reshape.146
  111.1 0.7 bitcast_reduce_fusion
  111.8 1.0 constant_dynamic-update-slice_fusion.2
  112.8 0.6 copy-done.2
  113.5 0.7 fusion.7
  114.2 0.6 pad_bitcast_fusion
  114.8 0.7 constant_dynamic-update-slice_fusion.1
  115.4 0.7 constant_dynamic-update-slice_fusion
  116.1 1.3 collective-permute-start.1
  117.4 5.1 %collective-permute-start = (f32[2560,128]{1,0:T(8,128)}, f32[2560,128]{1,0:T(8,128)}, u32[]{:S(2)}, u32[]{:S(2)}) collective-permute-start(f32[2560,128]{1,0:T(8,128)} %constant_dynamic-update-slice_fusion), channel_id=1, source_target_pairs={{0,2},{2,4},{4,6},{6,8},{8,10},{10,12},{12,14},{14,16},{16,18},{18... | collective-permute-start | bytes 3932168 | tf_op jit(solution)/shard_map/ppermute | solution.py:398
  122.5 0.6 slice_subtract_fusion
  123.1 21.3 %near1.1.before = f32[2048,128]{1,0:T(8,128)} custom-call(f32[2048,128]{1,0:T(8,128)} %get-tuple-element.13.own), custom_call_target="tpu_custom_call" | custom-call | flops 10000000000 | bytes 10000000 | tf_op jit(solution)/shard_map/near1/pallas_call | solution.py:368
  144.4 1.7 collective-permute-done.1.following
  146.1 1.0 fusion.11
  147.1 1.0 fusion.10
  148.2 8.6 %gather_fusion = f32[2048,256]{1,0:T(8,128)} fusion(f32[768,256]{1,0:T(8,128)S(1)} %maximum_maximum_fusion, s32[2048]{0:T(1024)S(1)} %broadcast_clamp_fusion), kind=kCustom, calls=%fused_computation | custom fusion | bytes 4202496 | tf_op jit(solution)/shard_map/jit(_take)/gather | solution.py:487
  156.8 5.9 %fusion = f32[256,16,168]{2,1,0:T(8,128)} fusion(f32[256,8,256]{2,1,0:T(8,128)} %bitcast.62, pred[256,8]{1,0:T(8,128)(4,1)S(1)} %copy.40, s32[256,8]{1,0:T(8,128)S(1)} %copy.39), kind=kOutput, calls=%fused_computation.2 | convolution fusion | flops 66437120 | bytes 4859904 | tf_op jit(solution)/shard_map/nje,njk->nke/dot_general | solution.py:489
  162.6 5.1 %copy.42 = f32[256,16,168]{0,2,1:T(8,128)} copy(f32[256,16,168]{2,1,0:T(8,128)} %fusion) | data formatting | bytes 5505024 | tf_op jit(solution)/shard_map/nje,njk->nke/dot_general | solution.py:489
  167.8 3.7 %fusion.13 = f32[256,3,56]{0,2,1:T(8,128)S(1)} fusion(f32[256,2688,1]{0,1,2:T(8,128)} %bitcast.60, f32[3,56,2688]{2,1,0:T(8,128)S(1)} %bitcast.63), kind=kOutput, calls=%fused_computation.43 | convolution fusion | flops 1387266048 | bytes 4730880 | tf_op jit(solution)/shard_map/dot_general | solution.py:490
  171.5 0.2 copy.55
  171.8 0.9 reshape.152.local
  172.8 31.8 %near2.1.near = f32[2048,128]{1,0:T(8,128)} custom-call(s32[512]{0:T(512)} %bitcast.80, f32[2560,128]{1,0:T(8,128)} %collective-permute-done.previous, f32[2560,128]{1,0:T(8,128)} %collective-permute-done.1.following, f32[2048,128]{1,0:T(8,128)} %get-tuple-element.13.own, f32[2048,128]{1,0:T(8,128)} %near1.1.before), custom_call_target="tpu_custom_call" | custom-call | flops 20000000000 | bytes 10000000 | tf_op jit(solution)/shard_map/near2/pallas_call | solution.py:380
  204.6 18.9 %all-gather.2.cloned.1.call-done = f32[2048,128]{1,0:T(8,128)} async-done(((f32[8,128]{1,0:T(8,128)}), f32[2048,128]{1,0:T(8,128)}) %all-gather.2.cloned.1.call-update) | async-done | bytes 1048592 | tf_op jit(solution)/shard_map/all_gather | solution.py:472
  223.4 1.3 slice.64
  224.8 0.3 convolution_bitcast_fusion
  225.1 3.2 convolution_bitcast_fusion.1
  228.3 1.2 fusion.14
  229.6 0.6 reshape.156.pushed
  230.2 33.2 %far.1 = f32[768,128]{1,0:T(8,128)} custom-call(s32[32768]{0:T(1024)} %bitcast.74, f32[768]{0:T(1024)} %reshape.139.centers, f32[2048,128]{1,0:T(8,128)} %get-tuple-element.13.own, f32[2048,128]{1,0:T(8,128)} %near2.1.near, f32[768,128]{1,0:T(8,128)} %reshape.152.local, f32[24,128]{1,0:T(8,128)} %reshape.156.pushed, f32[3,64,128]{2,1,0:T(8,128)} %broadcast_in_dim.26.surface, ...), custom_call_target="tpu_custom_call" | custom-call | tf_op jit(solution)/shard_map/far/pallas_call | solution.py:507
  263.4 28.5 %all_to_all.10 = f32[128,1,768]{2,1,0:T(1,128)} all-to-all(f32[128,1,768]{2,1,0:T(1,128)} %bitcast.67), channel_id=1, replica_groups=mesh['gx'=128,'gy'=2] {'gx'}, dimensions={0} | all-to-all | bytes 786432 | tf_op jit(solution)/shard_map/all_to_all | solution.py:363
  291.9 15.2 %back.1 = f32[204,128]{1,0:T(8,128)} custom-call(s32[8704]{0:T(1024)} %reduce.dest, f32[768,128]{1,0:T(8,128)} %bitcast.68), custom_call_target="tpu_custom_call" | custom-call | tf_op jit(solution)/shard_map/back/pallas_call | solution.py:521
  307.1 1.6 reshape.177
  (59 shorter events, 1.9 us)
Async XLA Ops:
  6.5 3.7 %copy-start = (f32[544,544]{1,0:T(8,128)S(1)}, f32[544,544]{1,0:T(8,128)}, u32[]{:S(2)}) copy-start(f32[544,544]{1,0:T(8,128)} %param.17) | copy-start | bytes 3551236
  8.8 2.7 copy-start.6
  11.1 1.5 copy-start.8
  14.3 30.3 %copy-start.11 = (f32[3,1,256]{2,1,0:T(1,128)S(1)}, f32[3,1,256]{2,1,0:T(1,128)}, u32[]{:S(2)}) copy-start(f32[3,1,256]{2,1,0:T(1,128)} %param.19) | copy-start | bytes 9220
  14.3 31.6 %copy-start.10 = (s32[1,8,256]{2,1,0:T(8,128)S(1)}, s32[1,8,256]{2,1,0:T(8,128)}, u32[]{:S(2)}) copy-start(s32[1,8,256]{2,1,0:T(8,128)} %param.22) | copy-start | bytes 24580
  14.3 32.0 %copy-start.9 = (s32[1,8,256]{2,1,0:T(8,128)S(1)}, s32[1,8,256]{2,1,0:T(8,128)}, u32[]{:S(2)}) copy-start(s32[1,8,256]{2,1,0:T(8,128)} %param.23) | copy-start | bytes 24580
  28.1 41.1 %all-to-all-start = ((f32[128,1,1536]{2,1,0:T(1,128)}), f32[128,1,1536]{2,1,0:T(1,128)S(1)}, u32[]{:S(2)}, u32[]{:S(2)}) async-start(f32[128,1,1536]{2,1,0:T(1,128)} %bitcast.65), calls=%async_computation | async-start | bytes 1572864 | tf_op jit(solution)/shard_map/all_to_all | solution.py:363
  44.5 179.0 %all-gather.2.cloned.1.call-start = ((), (), s32[]{:S(2)}) async-start(), calls=%async_computation.2 | async-start | bytes 1052672 | tf_op jit(solution)/shard_map/all_gather | solution.py:472
  49.6 61.5 %copy-start.7 = (f32[168,168]{1,0:T(8,128)S(1)}, f32[168,168]{1,0:T(8,128)}, u32[]{:S(2)}) copy-start(f32[168,168]{1,0:T(8,128)} %param.25) | copy-start | bytes 338692
  69.2 1.0 copy-start.5
  109.6 2.2 copy-start.4
  111.7 1.7 copy-start.2
  112.8 9.7 %copy-start.12 = (s32[1,3,256]{2,0,1:T(1,128)S(1)}, s32[1,3,256]{2,0,1:T(1,128)}, u32[]{:S(2)}) copy-start(s32[1,3,256]{2,0,1:T(1,128)} %param.21) | copy-start | bytes 9220
  116.1 30.0 %collective-permute-start.1 = (f32[2560,128]{1,0:T(8,128)}, f32[2560,128]{1,0:T(8,128)}, u32[]{:S(2)}, u32[]{:S(2)}) collective-permute-start(f32[2560,128]{1,0:T(8,128)} %constant_dynamic-update-slice_fusion), channel_id=1, source_target_pairs={{2,0},{4,2},{6,4},{8,6},{10,8},{12,10},{14,12},{16,14},{18,16},{20... | collective-permute-start | bytes 3932168 | tf_op jit(solution)/shard_map/ppermute | solution.py:398
  117.4 29.7 %collective-permute-start = (f32[2560,128]{1,0:T(8,128)}, f32[2560,128]{1,0:T(8,128)}, u32[]{:S(2)}, u32[]{:S(2)}) collective-permute-start(f32[2560,128]{1,0:T(8,128)} %constant_dynamic-update-slice_fusion), channel_id=1, source_target_pairs={{0,2},{2,4},{4,6},{6,8},{8,10},{10,12},{12,14},{14,16},{16,18},{18... | collective-permute-start | bytes 3932168 | tf_op jit(solution)/shard_map/ppermute | solution.py:398
  162.6 5.1 %copy-start.1 = (f32[168,2688]{1,0:T(8,128)S(1)}, f32[168,2688]{1,0:T(8,128)}, u32[]{:S(2)}) copy-start(f32[168,2688]{1,0:T(8,128)} %copy.43) | copy-start | bytes 5419012
  172.8 52.0 %copy-start.13 = (s32[1,1,256]{2,1,0:T(1,128)S(1)}, s32[1,1,256]{2,1,0:T(1,128)}, u32[]{:S(2)}) copy-start(s32[1,1,256]{2,1,0:T(1,128)} %param.24) | copy-start | bytes 3076
  225.1 3.2 %copy-start.3 = (f32[8,168,168]{2,1,0:T(8,128)S(1)}, f32[8,168,168]{2,1,0:T(8,128)}, u32[]{:S(2)}) copy-start(f32[8,168,168]{2,1,0:T(8,128)} %param.27) | copy-start | bytes 2709508
Sparse Core Ops, SparseCore 0:
  123.2 100.1 all-gather.1
